TPU v7x, 32 devices: a whole 2x2x4 slice. The times are simulated.
32 devices in a mesh: rows: 8 (over z, y), wide: 4 (over x, core).
Axes of the slice: x: 2, y: 2, z: 4, core: 2. Of those that a mesh axis runs over, the one named last changes fastest.
Arguments:
- tokens: bfloat16 [16, 1024, 1024], P('rows', 'wide'), may hold values from -6 to 6
- doc_ids: int32 [16, 1024], P('rows'), may hold values from 0 to 5, never falling along the last dimension, each value on 1 to 512 neighbouring positions
- factor_weight: bfloat16 [1024, 800], replicated, may hold values from -0.3125 to 0.3125
- output_weight: bfloat16 [1024, 1024], replicated, may hold values from -0.5 to 0.5
- norm_one: float32 [1024], replicated, may hold values from 0.5 to 1.5
- norm_two: float32 [1024], replicated, may hold values from 0.5 to 1.5
- gate_weight: bfloat16 [1024, 2816], P(None, 'wide'), may hold values from -0.1875 to 0.1875
- up_weight: bfloat16 [1024, 2816], P(None, 'wide'), may hold values from -0.1875 to 0.1875
- down_weight: bfloat16 [2816, 1024], P('wide'), may hold values from -0.15625 to 0.15625
- cotangent: bfloat16 [16, 1024, 1024], P('rows', 'wide'), may hold values from -6 to 6
Outputs:
- output: bfloat16 [16, 1024, 1024], P('rows', 'wide')
- input_grad: bfloat16 [16, 1024, 1024], P('rows', 'wide')
- grad_factors: float32 [1024, 800], replicated
- grad_out: float32 [1024, 1024], replicated
- grad_norm_one: float32 [1024], replicated
- grad_norm_two: float32 [1024], replicated
- grad_gate: float32 [1024, 2816], P(None, 'wide')
- up_weight_gradient: float32 [1024, 2816], P(None, 'wide')
- down_weight_gradient: float32 [2816, 1024], P('wide')
Inputs may be any that keep to these rules, and one draw needn't show every extreme that they name: `doc_ids`: in each sequence the ids never fall along the positions; a document holds 1 to 512 positions, and one document of every sequence holds exactly 512.
All inputs are finite; a program needn't handle non-finite values.
Results may differ from a plain program's by a relative error of at most 0.017.
The roundings to bfloat16 on the way count: a program that leaves them out, or rounds other values in their place, can miss the bound.
Values may be sent and summed in bfloat16 or wider, within the bound.
A program may use at most 256 MiB of HBM per device.

v0:
```python
import jax
import jax.numpy as jnp
from jax import lax
from jax.sharding import PartitionSpec as P

H = 16
DH = 64
RQ = 6
RK = 2
SEQ_BLOCK = 2


EPS = 1e-06
NEG = -1000000000.0
MATMUL_EXACTNESS = lax.Precision.HIGHEST


def expand(part_a, part_b, heads, rank):
    leading = part_a.shape[:-1]
    left_part = part_a.reshape(leading + (heads, rank))
    right_part = part_b.reshape(leading + (rank, -1))
    return (
        jnp.einsum("...hr,...rd->...hd", left_part, right_part, preferred_element_type=jnp.float32)
        / rank
    )


def factor_grads(grad_heads, part_a, part_b, heads, rank):
    leading = part_a.shape[:-1]
    left_part = part_a.reshape(leading + (heads, rank)).astype(jnp.float32)
    right_part = part_b.reshape(leading + (rank, -1)).astype(jnp.float32)
    grad_left = (
        jnp.einsum("...hd,...rd->...hr", grad_heads, right_part, precision=MATMUL_EXACTNESS) / rank
    )
    grad_right = (
        jnp.einsum("...hd,...hr->...rd", grad_heads, left_part, precision=MATMUL_EXACTNESS) / rank
    )
    return (grad_left.reshape(leading + (-1,)), grad_right.reshape(leading + (-1,)))


def split_query(factor_rows):
    cut_one = H * RQ
    return (factor_rows[..., :cut_one], factor_rows[..., cut_one:])


def split_pair(factor_rows):
    cut_one = H * RK
    cut_two = cut_one + RK * DH
    cut_three = cut_two + H * RK
    return (
        factor_rows[..., :cut_one],
        factor_rows[..., cut_one:cut_two],
        factor_rows[..., cut_two:cut_three],
        factor_rows[..., cut_three:],
    )


def block_scores(queries, key_heads, allowed):
    scores = jnp.einsum(
        "sqhd,skhd->shqk", queries, key_heads, preferred_element_type=jnp.float32
    ) * DH ** (-0.5)
    return jnp.where(allowed[:, None], scores, NEG)


def attend_forward(block_parts):
    queries, key_heads, value_heads, allowed = block_parts
    scores = block_scores(queries, key_heads, allowed)
    row_top = jnp.max(scores, axis=-1, keepdims=True)
    exponent = jnp.exp(scores - row_top)
    totals = jnp.sum(exponent, axis=-1, keepdims=True)
    attn_probs = (exponent / totals).astype(jnp.bfloat16)
    mixed_out = jnp.einsum(
        "shqk,skhd->sqhd", attn_probs, value_heads, preferred_element_type=jnp.float32
    )
    return (mixed_out.astype(jnp.bfloat16), (row_top + jnp.log(totals))[..., 0])


def attend_backward(block_parts):
    queries, key_heads, value_heads, allowed, logsum, grad_mixed = block_parts
    scores = block_scores(queries, key_heads, allowed)
    attn_probs = jnp.exp(scores - logsum[..., None])
    grad_probs = jnp.einsum(
        "sqhd,skhd->shqk", grad_mixed, value_heads, preferred_element_type=jnp.float32
    )
    inner_sum = jnp.sum(attn_probs * grad_probs, axis=-1, keepdims=True)
    grad_scores = (attn_probs * (grad_probs - inner_sum)).astype(jnp.bfloat16)
    scaling = DH ** (-0.5)
    grad_query = (
        jnp.einsum("shqk,skhd->sqhd", grad_scores, key_heads, preferred_element_type=jnp.float32)
        * scaling
    )
    grad_key = (
        jnp.einsum("shqk,sqhd->skhd", grad_scores, queries, preferred_element_type=jnp.float32)
        * scaling
    )
    grad_value = jnp.einsum(
        "shqk,sqhd->skhd",
        attn_probs.astype(jnp.bfloat16),
        grad_mixed,
        preferred_element_type=jnp.float32,
    )
    return (grad_query, grad_key, grad_value)


def grouped(array_in):
    return array_in.reshape((array_in.shape[0] // SEQ_BLOCK, SEQ_BLOCK) + array_in.shape[1:])


def ungrouped(array_in):
    return array_in.reshape((array_in.shape[0] * array_in.shape[1],) + array_in.shape[2:])


def norm_backward(grad_normed, values, scaling, gain):
    weighted = grad_normed * gain
    grad_values = scaling * weighted - values * (scaling * scaling * scaling) * jnp.mean(
        weighted * values, axis=-1, keepdims=True
    )
    grad_gain = jnp.sum(grad_normed * values * scaling, axis=(0, 1))
    return (grad_values, grad_gain)


def body(
    tokens,
    doc_ids,
    factor_weight,
    output_weight,
    norm_one,
    norm_two,
    gate_weight,
    up_weight,
    down_weight,
    cotangent,
):
    seq_count, own_len, _unused = tokens.shape
    full_len = doc_ids.shape[1]
    offset = lax.axis_index("wide") * own_len
    query_columns = H * RQ + RQ * DH
    hidden_in = tokens.astype(jnp.float32)
    scale_one = lax.rsqrt(jnp.mean(hidden_in * hidden_in, axis=-1, keepdims=True) + EPS)
    first_normalized = (hidden_in * scale_one * norm_one).astype(jnp.bfloat16)
    normalized_total = lax.all_gather(first_normalized, "wide", axis=1, tiled=True)
    query_fac = jnp.einsum(
        "cnx,xo->cno",
        first_normalized,
        factor_weight[:, :query_columns],
        preferred_element_type=jnp.float32,
    ).astype(jnp.bfloat16)
    pair_fac = jnp.einsum(
        "cnx,xo->cno",
        normalized_total,
        factor_weight[:, query_columns:],
        preferred_element_type=jnp.float32,
    ).astype(jnp.bfloat16)
    query_a, query_b = split_query(query_fac)
    key_a, key_b, value_a, value_b = split_pair(pair_fac)
    queries = expand(query_a, query_b, H, RQ).astype(jnp.bfloat16)
    key_heads = expand(key_a, key_b, H, RK).astype(jnp.bfloat16)
    value_heads = expand(value_a, value_b, H, RK).astype(jnp.bfloat16)
    doc_query = lax.dynamic_slice_in_dim(doc_ids, offset, own_len, 1)
    key_pos = lax.broadcasted_iota(jnp.int32, (own_len, full_len), 1)
    query_pos = lax.broadcasted_iota(jnp.int32, (own_len, full_len), 0) + offset
    allowed = (doc_query[:, :, None] == doc_ids[:, None, :]) & (key_pos <= query_pos)[None]
    mixed_out, logsum = lax.map(
        attend_forward,
        (grouped(queries), grouped(key_heads), grouped(value_heads), grouped(allowed)),
    )
    attention_result = ungrouped(mixed_out).reshape(seq_count, own_len, H * DH)
    logsum = ungrouped(logsum)
    residual_branch = jnp.einsum(
        "trq,qx->trx", attention_result, output_weight, preferred_element_type=jnp.float32
    )
    hidden_middle = hidden_in + residual_branch
    scale_two = lax.rsqrt(jnp.mean(hidden_middle * hidden_middle, axis=-1, keepdims=True) + EPS)
    second_normalized = (hidden_middle * scale_two * norm_two).astype(jnp.bfloat16)
    input_rows_total = lax.all_gather(second_normalized, "wide", axis=1, tiled=True)
    gate_logits = jnp.einsum(
        "cnx,xo->cno", input_rows_total, gate_weight, preferred_element_type=jnp.float32
    )
    up_activation = jnp.einsum(
        "cnx,xo->cno", input_rows_total, up_weight, preferred_element_type=jnp.float32
    )
    gate_sig = jax.nn.sigmoid(gate_logits)
    feedforward_hidden = (gate_logits * gate_sig * up_activation).astype(jnp.bfloat16)
    partial_output = jnp.einsum(
        "gxk,km->gxm", feedforward_hidden, down_weight, preferred_element_type=jnp.float32
    )
    feed_out = lax.psum_scatter(
        partial_output.astype(jnp.bfloat16), "wide", scatter_dimension=1, tiled=True
    ).astype(jnp.float32)
    gradient_total = lax.all_gather(cotangent, "wide", axis=1, tiled=True)
    hidden_gradient = jnp.einsum(
        "uow,nw->uon", gradient_total, down_weight, preferred_element_type=jnp.float32
    )
    gate_logits_gradient = (
        hidden_gradient * up_activation * gate_sig * (1.0 + gate_logits * (1.0 - gate_sig))
    ).astype(jnp.bfloat16)
    up_logits_gradient = (hidden_gradient * gate_logits * gate_sig).astype(jnp.bfloat16)
    grad_in_part = jnp.einsum(
        "hnc,uc->hnu", gate_logits_gradient, gate_weight, preferred_element_type=jnp.float32
    )
    grad_in_part = grad_in_part + jnp.einsum(
        "hnc,uc->hnu", up_logits_gradient, up_weight, preferred_element_type=jnp.float32
    )
    grad_normed_two = lax.psum_scatter(
        grad_in_part.astype(jnp.bfloat16), "wide", scatter_dimension=1, tiled=True
    ).astype(jnp.float32)
    grad_gate = jnp.einsum(
        "wvm,wvu->mu", input_rows_total, gate_logits_gradient, preferred_element_type=jnp.float32
    )
    up_weight_gradient = jnp.einsum(
        "wvm,wvu->mu", input_rows_total, up_logits_gradient, preferred_element_type=jnp.float32
    )
    down_weight_gradient = jnp.einsum(
        "qmw,qmv->wv", feedforward_hidden, gradient_total, preferred_element_type=jnp.float32
    )
    grad_gate, up_weight_gradient, down_weight_gradient = (
        lax.psum(grad_gate.astype(jnp.bfloat16), "rows").astype(jnp.float32),
        lax.psum(up_weight_gradient.astype(jnp.bfloat16), "rows").astype(jnp.float32),
        lax.psum(down_weight_gradient.astype(jnp.bfloat16), "rows").astype(jnp.float32),
    )
    output = (hidden_middle + feed_out).astype(jnp.bfloat16)
    grad_mid_norm, gain_two = norm_backward(grad_normed_two, hidden_middle, scale_two, norm_two)
    grad_mid = cotangent.astype(jnp.float32) + grad_mid_norm
    branch_gradient = grad_mid.astype(jnp.bfloat16)
    grad_w_out = jnp.einsum(
        "amx,amb->xb", attention_result, branch_gradient, preferred_element_type=jnp.float32
    )
    grad_attended = jnp.einsum(
        "pjk,zk->pjz", branch_gradient, output_weight, preferred_element_type=jnp.float32
    ).astype(jnp.bfloat16)
    grad_attended = grad_attended.reshape(seq_count, own_len, H, DH)
    grad_query, grad_key, grad_value = lax.map(
        attend_backward,
        (
            grouped(queries),
            grouped(key_heads),
            grouped(value_heads),
            grouped(allowed),
            grouped(logsum),
            grouped(grad_attended),
        ),
    )
    grad_query = ungrouped(grad_query)
    grad_key = ungrouped(grad_key)
    grad_value = ungrouped(grad_value)
    grad_qa, grad_qb = factor_grads(grad_query, query_a, query_b, H, RQ)
    grad_ka, grad_kb = factor_grads(grad_key, key_a, key_b, H, RK)
    grad_va, grad_vb = factor_grads(grad_value, value_a, value_b, H, RK)
    pair_grads = jnp.concatenate([grad_ka, grad_kb, grad_va, grad_vb], axis=-1)
    pair_own = lax.psum_scatter(
        pair_grads.astype(jnp.bfloat16), "wide", scatter_dimension=1, tiled=True
    ).astype(jnp.float32)
    factor_gradient = jnp.concatenate([grad_qa, grad_qb, pair_own], axis=-1).astype(jnp.bfloat16)
    grad_w_factors = jnp.einsum(
        "wvm,wvu->mu", first_normalized, factor_gradient, preferred_element_type=jnp.float32
    )
    grad_normed_one = jnp.einsum(
        "hnc,uc->hnu", factor_gradient, factor_weight, preferred_element_type=jnp.float32
    )
    grad_in_norm, gain_one = norm_backward(grad_normed_one, hidden_in, scale_one, norm_one)
    input_grad = (grad_mid + grad_in_norm).astype(jnp.bfloat16)
    grad_w_factors, grad_w_out, gain_one, gain_two = lax.psum(
        (grad_w_factors, grad_w_out, gain_one, gain_two), ("rows", "wide")
    )
    return (
        output,
        input_grad,
        grad_w_factors,
        grad_w_out,
        gain_one,
        gain_two,
        grad_gate,
        up_weight_gradient,
        down_weight_gradient,
    )


def solution(mesh):
    placed = (
        P("rows", "wide", None),
        P("rows", None),
        P(),
        P(),
        P(),
        P(),
        P(None, "wide"),
        P(None, "wide"),
        P("wide", None),
        P("rows", "wide", None),
    )
    return jax.shard_map(
        body,
        mesh=mesh,
        in_specs=placed,
        out_specs=(
            P("rows", "wide", None),
            P("rows", "wide", None),
            P(),
            P(),
            P(),
            P(),
            P(None, "wide"),
            P(None, "wide"),
            P("wide", None),
        ),
        check_vma=False,
    )
```

profile of v0, /device:TPU:0, one launch (start us, length us, event | category | flops | bytes accessed | tf_op | source)
XLA Modules:
  0.0 899.3 jit_solution(4847978893055860476)
XLA Ops:
  29.6 20.3 %all-gather.4.cloned.1.call-done = bf16[2,1024,1024]{2,1,0:T(8,128)(2,1)} async-done(((bf16[2,256,1024]{2,1,0:T(8,128)(2,1)}), bf16[2,1024,1024]{2,1,0:T(8,128)(2,1)}) %all-gather.4.cloned.1.call-update) | async-done | bytes 4194320 | tf_op jit(solution)/shard_map/all_gather | solution.py:141
  67.3 12.8 %copy.94 = f32[2,1024,16,64]{1,3,2,0:T(8,128)} copy(f32[2,1024,16,64]{3,2,1,0:T(8,128)} %fusion.68) | data formatting | bytes 16777216 | tf_op jit(solution)/shard_map/...hr,...rd->...hd/dot_general | solution.py:23
  92.5 12.8 %copy.87 = f32[2,1024,16,64]{1,3,2,0:T(8,128)} copy(f32[2,1024,16,64]{3,2,1,0:T(8,128)} %fusion.66) | data formatting | bytes 16777216 | tf_op jit(solution)/shard_map/...hr,...rd->...hd/dot_general | solution.py:23
  105.3 17.1 %fusion.65 = (f32[2,16,256]{2,1,0:T(8,128)S(1)}, f32[2,16,256,1024]{3,2,1,0:T(8,128)}) fusion(f32[2,1024,16,64]{1,3,2,0:T(8,128)} %copy.94, f32[2,256,16,64]{1,3,2,0:T(8,128)} %copy.91, pred[2,256,1024]{2,1,0:T(8,128)(4,1)} %compare_and_fusion), kind=kOutput, calls=%fused_computation.112 | convolution fusion | flops 1104142336 | bytes 44597248 | tf_op jit(solution)/shard_map/while/body/eval_jaxpr/sqhd,skhd->shqk/dot_general | solution.py:59
  122.4 14.7 %fusion = f32[2,16,256]{2,1,0:T(8,128)S(1)} fusion(f32[2,16,256,1024]{3,2,1,0:T(8,128)} %get-tuple-element.85, f32[2,16,256]{2,1,0:T(8,128)S(1)} %get-tuple-element.84), kind=kLoop, calls=%fused_computation.6 | loop fusion | flops 16769024 | bytes 33619968 | tf_op jit(solution)/shard_map/while/body/eval_jaxpr/reduce_sum | solution.py:70
  137.1 13.2 %fusion.38 = bf16[2,16,64,256]{3,2,1,0:T(8,128)(2,1)S(1)} fusion(f32[2,16,256,1024]{3,2,1,0:T(8,128)} %get-tuple-element.85, f32[2,16,256]{2,1,0:T(8,128)S(1)} %fusion, f32[2,16,256]{2,1,0:T(8,128)S(1)} %get-tuple-element.84, f32[2,1024,16,64]{1,3,2,0:T(8,128)S(1)} %copy-done.4), kind=kOutput, calls=%fused_computation.67 | convolution fusion | flops 1103626240 | bytes 43057152 | tf_op jit(solution)/shard_map/while/body/eval_jaxpr/shqk,skhd->sqhd/dot_general | solution.py:72
  155.1 33.8 %all-gather.6.cloned.1.call-done = bf16[2,1024,1024]{2,1,0:T(8,128)(2,1)} async-done(((bf16[2,256,1024]{2,1,0:T(8,128)(2,1)}), bf16[2,1024,1024]{2,1,0:T(8,128)(2,1)}) %all-gather.6.cloned.1.call-update) | async-done | bytes 4194320 | tf_op jit(solution)/shard_map/all_gather | solution.py:175
  202.4 22.6 %all-gather.8.cloned.1.call-done = bf16[2,1024,1024]{2,1,0:T(8,128)(2,1)} async-done(((bf16[2,256,1024]{2,1,0:T(8,128)(2,1)}), bf16[2,1024,1024]{2,1,0:T(8,128)(2,1)}) %all-gather.8.cloned.1.call-update) | async-done | bytes 4194320 | tf_op jit(solution)/shard_map/all_gather | solution.py:190
  225.0 10.3 %multiply_convert_fusion.3 = (bf16[2,1024,704]{1,2,0:T(8,128)(2,1)S(1)}, bf16[2,1024,704]{1,2,0:T(8,128)(2,1)S(1)}, bf16[2,1024,704]{1,2,0:T(8,128)(2,1)}) fusion(f32[2,1024,704]{1,2,0:T(8,128)} %fusion.47, f32[2,1024,704]{1,2,0:T(8,128)} %fusion.43, bf16[2,1024,1024]{2,1,0:T(8,128)(2,1)} %all-gather.8.cloned.1.call-done, bf16[704,1024]{1,0:T(8,128)(2,1)} %param.18), kind=kOutput, calls=%fused_computation.15 | convolution fusion | flops 2975858688 | bytes 25821184 | tf_op jit(solution)/shard_map/uow,nw->uon/dot_general | solution.py:191
  252.1 36.6 %reduce-scatter.6.cloned.1.call-done = bf16[2,256,1024]{2,1,0:T(8,128)(2,1)} async-done(((bf16[2,1024,1024]{2,1,0:T(8,128)(2,1)}), bf16[2,256,1024]{2,1,0:T(8,128)(2,1)}) %reduce-scatter.6.cloned.1.call-update) | async-done | bytes 1048592 | tf_op jit(solution)/shard_map/reduce_scatter | solution.py:204
  291.9 43.8 %reduce-scatter.4.cloned.1.call-done = bf16[2,256,1024]{2,1,0:T(8,128)(2,1)} async-done(((bf16[2,1024,1024]{2,1,0:T(8,128)(2,1)}), bf16[2,256,1024]{2,1,0:T(8,128)(2,1)}) %reduce-scatter.4.cloned.1.call-update) | async-done | bytes 1048592 | tf_op jit(solution)/shard_map/reduce_scatter | solution.py:187
  343.1 25.8 %multiply_reduce_fusion = (f32[2,16,256]{2,1,0:T(8,128)S(1)}, f32[2,16,256,1024]{3,2,1,0:T(8,128)}) fusion(f32[2,16,256,1024]{3,2,1,0:T(8,128)} %get-tuple-element.85, f32[2,16,256]{2,1,0:T(8,128)S(1)} %log_add_fusion, bf16[2,256,16,64]{1,3,2,0:T(8,128)(2,1)S(1)} %bitcast.112, f32[2,1024,16,64]{1,3,2,0:T(8,128)} %copy.87), kind=kOutput, calls=%fused_computation.1 | convolution fusion | flops 1103093760 | bytes 76611584 | tf_op jit(solution)/shard_map/while/body/eval_jaxpr/sqhd,skhd->shqk/dot_general | solution.py:82
  368.9 27.9 %multiply_convert_fusion = bf16[2,16,256,1024]{3,2,1,0:T(8,128)(2,1)} fusion(f32[2,16,256,1024]{3,2,1,0:T(8,128)} %get-tuple-element.89, f32[2,16,256,1024]{3,2,1,0:T(8,128)} %get-tuple-element.85, f32[2,16,256]{2,1,0:T(8,128)S(1)} %get-tuple-element.88, f32[2,16,256]{2,1,0:T(8,128)S(1)} %log_add_fusion), kind=kLoop, calls=%fused_computation | loop fusion | flops 33554432 | bytes 83951616 | tf_op jit(solution)/shard_map/while/body/eval_jaxpr/convert_element_type | solution.py:86
  396.8 12.0 %multiply_bitcast_fusion = f32[2,1024,16,64]{1,3,2,0:T(8,128)} fusion(bf16[2,16,256,1024]{3,2,1,0:T(8,128)(2,1)} %multiply_convert_fusion, f32[2,256,16,64]{1,3,2,0:T(8,128)S(1)} %copy-done.6), kind=kOutput, calls=%fused_computation.11 | convolution fusion | flops 1076887552 | bytes 27262976 | tf_op jit(solution)/shard_map/while/body/eval_jaxpr/shqk,sqhd->skhd/dot_general | solution.py:93
  408.9 14.6 %copy.104 = f32[2,1024,16,64]{3,2,1,0:T(8,128)} copy(f32[2,1024,16,64]{1,3,2,0:T(8,128)} %multiply_bitcast_fusion) | data formatting | bytes 16777216 | tf_op jit(solution)/shard_map/while/body/eval_jaxpr/mul | solution.py:93
  423.5 17.1 %fusion.70 = f32[2,1024,16,2]{2,3,1,0:T(2,128)} fusion(f32[2,1024,16,64]{3,2,1,0:T(8,128)} %copy.104, bf16[2,1024,2,64]{3,2,1,0:T(2,128)(2,1)S(1)} %copy-done.14), kind=kOutput, calls=%fused_computation.117 | convolution fusion | flops 50331648 | bytes 9175040 | tf_op jit(solution)/shard_map/...hd,...rd->...hr/dot_general | solution.py:33
  450.3 16.8 %fusion.6 = f32[2,1024,16,64]{1,3,2,0:T(8,128)} fusion(bf16[2,256,16,64]{1,3,2,0:T(8,128)(2,1)S(1)} %bitcast.113, f32[2,16,256,1024]{3,2,1,0:T(8,128)} %get-tuple-element.85, f32[2,16,256]{2,1,0:T(8,128)S(1)} %log_add_fusion), kind=kOutput, calls=%fused_computation.25 | convolution fusion | flops 1090519040 | bytes 43024384 | tf_op jit(solution)/shard_map/while/body/eval_jaxpr/shqk,sqhd->skhd/dot_general | solution.py:96
  467.1 14.6 %copy.111 = f32[2,1024,16,64]{3,2,1,0:T(8,128)} copy(f32[2,1024,16,64]{1,3,2,0:T(8,128)} %fusion.6) | data formatting | bytes 16777216 | tf_op jit(solution)/shard_map/while/body/eval_jaxpr/shqk,sqhd->skhd/transpose | solution.py:96
  481.7 17.1 %fusion.72 = f32[2,1024,16,2]{2,3,1,0:T(2,128)} fusion(f32[2,1024,16,64]{3,2,1,0:T(8,128)} %copy.111, bf16[2,1024,2,64]{3,2,1,0:T(2,128)(2,1)S(1)} %copy-done.12), kind=kOutput, calls=%fused_computation.119 | convolution fusion | flops 50331648 | bytes 9175040 | tf_op jit(solution)/shard_map/...hd,...rd->...hr/dot_general | solution.py:33
  498.8 9.8 %fusion.73 = f32[2,1024,2,64]{3,2,1,0:T(2,128)} fusion(bf16[2,1024,16,2]{2,3,1,0:T(2,128)(2,1)S(1)} %copy-done.16, f32[2,1024,16,64]{3,2,1,0:T(8,128)S(1)} %copy-done.3), kind=kOutput, calls=%fused_computation.120 | convolution fusion | flops 50331648 | bytes 9568256 | tf_op jit(solution)/shard_map/...hd,...hr->...rd/dot_general | solution.py:36
  535.7 12.4 %multiply_bitcast_fusion.1 = f32[2,256,16,64]{1,3,2,0:T(8,128)} fusion(bf16[2,16,256,1024]{3,2,1,0:T(8,128)(2,1)} %multiply_convert_fusion, f32[2,1024,16,64]{1,3,2,0:T(8,128)} %copy.94), kind=kOutput, calls=%fused_computation.55 | convolution fusion | flops 1078460416 | bytes 27262976 | tf_op jit(solution)/shard_map/while/body/eval_jaxpr/shqk,skhd->sqhd/dot_general | solution.py:89
  576.8 133.3 %all-reduce.8.cloned.1.call-done = (bf16[1024,704]{0,1:T(8,128)(2,1)}, bf16[1024,704]{0,1:T(8,128)(2,1)}, bf16[704,1024]{1,0:T(8,128)(2,1)}) async-done(((bf16[1024,704]{0,1:T(8,128)(2,1)}, bf16[1024,704]{0,1:T(8,128)(2,1)}, bf16[704,1024]{1,0:T(8,128)(2,1)}), (bf16[1024,704]{0,1:T(8,128)(2,1)}, bf16[1024,704]{0,1:T(8,128)(2,1)}, bf16[704,1024]{1,0:T(8,128)(2,1)})) %all-reduce.8.cloned.1.call-update) | async-done | bytes 4325392 | tf_op jit(solution)/shard_map/psum | solution.py:217
  721.2 40.9 %all-reduce = (f32[1024]{0:T(1024)}, f32[1024]{0:T(1024)}) all-reduce(f32[1024]{0:T(1024)S(1)} %get-tuple-element.52, f32[1024]{0:T(1024)S(1)} %copy-done.34), channel_id=1, replica_groups=mesh['rows'=8,'wide'=4] {'rows','wide'}, use_global_device_ids=true, to_apply=%region_13.14 | all-reduce | flops 2048 | bytes 16384 | tf_op jit(solution)/shard_map/psum | solution.py:262
  765.9 120.0 %all-reduce.6.cloned.1.call-done = (f32[1024,800]{0,1:T(8,128)}, f32[1024,1024]{1,0:T(8,128)}) async-done(((f32[1024,800]{0,1:T(8,128)}, f32[1024,1024]{1,0:T(8,128)}), (f32[1024,800]{0,1:T(8,128)}, f32[1024,1024]{1,0:T(8,128)})) %all-reduce.6.cloned.1.call-update) | async-done | bytes 7471120 | tf_op jit(solution)/shard_map/psum | solution.py:262
  (192 shorter events, 183.7 us)
Async XLA Ops:
  7.2 143.2 %copy-start = (bf16[1024,1024]{1,0:T(8,128)(2,1)S(1)}, bf16[1024,1024]{1,0:T(8,128)(2,1)}, u32[]{:S(2)}) copy-start(bf16[1024,1024]{1,0:T(8,128)(2,1)} %param.13) | copy-start | bytes 6291460
  7.2 42.7 %all-gather.4.cloned.1.call-start = ((), (), s32[]{:S(2)}) async-start(), calls=%async_computation.3 | async-start | bytes 5242880 | tf_op jit(solution)/shard_map/all_gather | solution.py:141
  12.6 176.3 %all-gather.6.cloned.1.call-start = ((), (), s32[]{:S(2)}) async-start(), calls=%async_computation.4 | async-start | bytes 5242880 | tf_op jit(solution)/shard_map/all_gather | solution.py:175
  57.3 10.0 %copy-start.13 = (bf16[2,1024,2,64]{3,2,1,0:T(2,128)(2,1)}, bf16[2,1024,2,64]{3,2,1,0:T(2,128)(2,1)S(1)}, u32[]{:S(2)}) copy-start(bf16[2,1024,2,64]{3,2,1,0:T(2,128)(2,1)S(1)} %copy.93) | copy-start | bytes 1572868
  82.4 10.0 %copy-start.11 = (bf16[2,1024,2,64]{3,2,1,0:T(2,128)(2,1)}, bf16[2,1024,2,64]{3,2,1,0:T(2,128)(2,1)S(1)}, u32[]{:S(2)}) copy-start(bf16[2,1024,2,64]{3,2,1,0:T(2,128)(2,1)S(1)} %copy.86) | copy-start | bytes 1572868
  122.4 14.7 %copy-start.4 = (f32[2,1024,16,64]{1,3,2,0:T(8,128)S(1)}, f32[2,1024,16,64]{1,3,2,0:T(8,128)}, u32[]{:S(2)}) copy-start(f32[2,1024,16,64]{1,3,2,0:T(8,128)} %copy.87) | copy-start | bytes 25165828
  137.1 13.2 %copy-start.7 = (bf16[2,256,1024]{2,1,0:T(8,128)(2,1)S(1)}, bf16[2,256,1024]{2,1,0:T(8,128)(2,1)}, u32[]{:S(2)}) copy-start(bf16[2,256,1024]{2,1,0:T(8,128)(2,1)} %param.10) | copy-start | bytes 3145732
  154.3 70.7 %all-gather.8.cloned.1.call-start = ((), (), s32[]{:S(2)}) async-start(), calls=%async_computation.6 | async-start | bytes 5242880 | tf_op jit(solution)/shard_map/all_gather | solution.py:190
  155.0 133.7 %reduce-scatter.6.cloned.1.call-start = ((), (), s32[]{:S(2)}) async-start(), calls=%async_computation.7 | async-start | bytes 5242880 | tf_op jit(solution)/shard_map/reduce_scatter | solution.py:204
  225.0 10.4 %copy-start.43 = (bf16[1024,704]{0,1:T(8,128)(2,1)S(1)}, bf16[1024,704]{0,1:T(8,128)(2,1)}, u32[]{:S(2)}) copy-start(bf16[1024,704]{0,1:T(8,128)(2,1)} %param.16) | copy-start | bytes 4325380
  244.0 91.7 %reduce-scatter.4.cloned.1.call-start = ((), (), s32[]{:S(2)}) async-start(), calls=%async_computation.5 | async-start | bytes 5242880 | tf_op jit(solution)/shard_map/reduce_scatter | solution.py:187
  252.0 83.7 %copy-start.25 = (bf16[2,256,1024]{2,1,0:T(8,128)(2,1)S(1)}, bf16[2,256,1024]{2,1,0:T(8,128)(2,1)}, u32[]{:S(2)}) copy-start(bf16[2,256,1024]{2,1,0:T(8,128)(2,1)} %param.19) | copy-start | bytes 3145732
  252.0 321.1 %reduce-scatter.8.cloned.1.call-start = ((), (), s32[]{:S(2)}) async-start(), calls=%async_computation.8 | async-start | bytes 1638400 | tf_op jit(solution)/shard_map/reduce_scatter | solution.py:250
  343.1 25.8 %copy-start.9 = (bf16[2,256,1024]{1,2,0:T(8,128)(2,1)}, bf16[2,256,1024]{1,2,0:T(8,128)(2,1)S(1)}, u32[]{:S(2)}) copy-start(bf16[2,256,1024]{1,2,0:T(8,128)(2,1)S(1)} %copy.96) | copy-start | bytes 3145732
  368.9 27.9 %copy-start.6 = (f32[2,256,16,64]{1,3,2,0:T(8,128)S(1)}, f32[2,256,16,64]{1,3,2,0:T(8,128)}, u32[]{:S(2)}) copy-start(f32[2,256,16,64]{1,3,2,0:T(8,128)} %copy.91) | copy-start | bytes 6291460
  408.8 14.7 %copy-start.14 = (bf16[2,1024,2,64]{3,2,1,0:T(2,128)(2,1)S(1)}, bf16[2,1024,2,64]{3,2,1,0:T(2,128)(2,1)}, u32[]{:S(2)}) copy-start(bf16[2,1024,2,64]{3,2,1,0:T(2,128)(2,1)} %copy-done.13) | copy-start | bytes 1572868
  423.5 17.2 %copy-start.2 = (f32[2,1024,16,64]{3,2,1,0:T(8,128)S(1)}, f32[2,1024,16,64]{3,2,1,0:T(8,128)}, u32[]{:S(2)}) copy-start(f32[2,1024,16,64]{3,2,1,0:T(8,128)} %copy.104) | copy-start | bytes 25165828
  423.5 17.2 %copy-start.15 = (bf16[2,1024,16,2]{2,3,1,0:T(2,128)(2,1)S(1)}, bf16[2,1024,16,2]{2,3,1,0:T(2,128)(2,1)}, u32[]{:S(2)}) copy-start(bf16[2,1024,16,2]{2,3,1,0:T(2,128)(2,1)} %copy.92) | copy-start | bytes 393220
  467.1 14.6 %copy-start.12 = (bf16[2,1024,2,64]{3,2,1,0:T(2,128)(2,1)S(1)}, bf16[2,1024,2,64]{3,2,1,0:T(2,128)(2,1)}, u32[]{:S(2)}) copy-start(bf16[2,1024,2,64]{3,2,1,0:T(2,128)(2,1)} %copy-done.11) | copy-start | bytes 1572868
  481.7 17.1 %copy-start.3 = (f32[2,1024,16,64]{3,2,1,0:T(8,128)S(1)}, f32[2,1024,16,64]{3,2,1,0:T(8,128)}, u32[]{:S(2)}) copy-start(f32[2,1024,16,64]{3,2,1,0:T(8,128)} %copy.111) | copy-start | bytes 25165828
  481.7 17.1 %copy-start.16 = (bf16[2,1024,16,2]{2,3,1,0:T(2,128)(2,1)S(1)}, bf16[2,1024,16,2]{2,3,1,0:T(2,128)(2,1)}, u32[]{:S(2)}) copy-start(bf16[2,1024,16,2]{2,3,1,0:T(2,128)(2,1)} %copy.85) | copy-start | bytes 393220
  519.6 190.5 %all-reduce.8.cloned.1.call-start = ((), (), s32[]{:S(2)}) async-start(), calls=%async_computation.10 | async-start | bytes 8650752 | tf_op jit(solution)/shard_map/psum | solution.py:217
  535.7 350.3 %all-reduce.6.cloned.1.call-start = ((), (), s32[]{:S(2)}) async-start(), calls=%async_computation.9 | async-start | bytes 14942208 | tf_op jit(solution)/shard_map/psum | solution.py:262
  718.3 43.8 %copy-start.37 = (f32[2,256]{1,0:T(2,128)S(1)}, f32[2,256]{1,0:T(2,128)}, u32[]{:S(2)}) copy-start(f32[2,256]{1,0:T(2,128)} %get-tuple-element.80) | copy-start | bytes 6148
  (34 other events, 140.1 us)
Sparse Core Ops, SparseCore 0:
  12.7 37.1 all-gather.3
  154.4 34.4 all-gather.5
  190.5 34.4 all-gather.7
  244.1 44.5 reduce-scatter.5
  291.1 44.5 reduce-scatter.3
  519.7 26.4 reduce-scatter.7
  550.6 159.4 all-reduce.7
  716.7 169.1 all-reduce.5
where the time goes:
time: 904 us; the launch traced here: 899 us
  waiting for transfers between devices  411 us (45%)
  matrix products  259 us (29%)
  local copies, waits for them, and re-layouts  102 us (11%)
  other arithmetic  71.4 us (8%)
  blocking collectives  40.9 us (5%)
  between operations  14.9 us (2%)
    psum x1, waiting for transfers between devices, body(): lax.psum(grad_gate.astype(jnp.bfloat16), 'rows').astype(jnp.float32)  133 us
    psum x1, waiting for transfers between devices, body(): lax.psum((grad_w_factors, grad_w_out, gain_one, gain_two), ('rows', 'wide'))  120 us
    reduce_scatter x1, waiting for transfers between devices, body(): lax.psum_scatter(partial_output.astype(jnp.bfloat16), 'wide', scatter_dim...  43.8 us
    dot_general x3, matrix products, factor_grads(): jnp.einsum('...hd,...rd->...hr', grad_heads, right_part, precision=MATMUL...  41.1 us
    psum x1, blocking collectives, body(): lax.psum((grad_w_factors, grad_w_out, gain_one, gain_two), ('rows', 'wide'))  40.9 us
    reduce_scatter x1, waiting for transfers between devices, body(): lax.psum_scatter(grad_in_part.astype(jnp.bfloat16), 'wide', scatter_dimen...  36.6 us
    all_gather x1, waiting for transfers between devices, body(): lax.all_gather(second_normalized, 'wide', axis=1, tiled=True)  33.8 us
    dot_general x3, local copies, waits for them, and re-layouts, expand(): jnp.einsum('...hr,...rd->...hd', left_part, right_part, preferred_element...  31 us
  transfers between devices with their start and end apart: 8, of which 7 were waited for; matrix products, arithmetic and copies ran while one was open for 12% of the time, Pallas kernels for 0%

commit v1 on v0

v1 whole, which is shorter than its diff:
```python
import functools

import jax
import jax.numpy as jnp
from jax import lax
from jax.experimental import pallas as pl
from jax.experimental.pallas import tpu as pltpu
from jax.sharding import PartitionSpec as P

H = 16
DH = 64
RQ = 6
RK = 2
MAX_DOC = 512
EPS = 1e-06
NEG = -1000000000.0
BIG = 3.0e38

QA = H * RQ
QCOLS = QA + RQ * DH
KA = H * RK
KCOLS = KA + RK * DH
KV = 2 * KCOLS
QPAD = 512
KPAD = 384
PAIRS = H // 2

F32 = jnp.float32
BF16 = jnp.bfloat16

NN = (((1,), (0,)), ((), ()))
NT = (((1,), (1,)), ((), ()))
TN = (((0,), (0,)), ((), ()))


def mm(a, b, dims=NN):
    return lax.dot_general(a, b, dims, preferred_element_type=F32)


def params(vmem_mb=60):
    return pltpu.CompilerParams(vmem_limit_bytes=vmem_mb << 20)


def cost(flops, nbytes):
    return pl.CostEstimate(flops=int(flops), bytes_accessed=int(nbytes), transcendentals=0)


def selection(shape, rule):
    row = lax.broadcasted_iota(jnp.int32, shape, 0)
    col = lax.broadcasted_iota(jnp.int32, shape, 1)
    return jnp.where(rule(row, col), 1.0, 0.0).astype(BF16)


def head_spread(pair, base, rank, shape):
    def rule(row, col):
        r = col // 128
        lane = col - r * 128
        head = 2 * pair + jnp.where(lane >= DH, 1, 0)
        return row == base + head * rank + r

    return selection(shape, rule)


def rank_tile(base, shape):
    def rule(row, col):
        r = col // 128
        lane = col - r * 128
        return row == base + r * DH + jnp.where(lane >= DH, lane - DH, lane)

    return selection(shape, rule)


def front_kernel(x_ref, w_ref, g_ref, n_ref, q_ref, kv_ref):
    x = x_ref[...].astype(F32)
    r = lax.rsqrt(jnp.mean(x * x, axis=-1, keepdims=True) + EPS)
    n = (x * r * g_ref[...]).astype(BF16)
    n_ref[...] = n
    f = mm(n, w_ref[...]).astype(BF16)
    q_ref[...] = f[:, :QPAD]
    kv_ref[:, :KV] = f[:, QCOLS:]
    kv_ref[:, KV:] = jnp.zeros((f.shape[0], KPAD - KV), BF16)


def front(x, w, gain):
    rows, d = x.shape
    blk = 256 if rows % 256 == 0 else rows
    return pl.pallas_call(
        front_kernel,
        grid=(rows // blk,),
        in_specs=[
            pl.BlockSpec((blk, d), lambda i: (i, 0)),
            pl.BlockSpec(w.shape, lambda i: (0, 0)),
            pl.BlockSpec((1, d), lambda i: (0, 0)),
        ],
        out_specs=[
            pl.BlockSpec((blk, d), lambda i: (i, 0)),
            pl.BlockSpec((blk, QPAD), lambda i: (i, 0)),
            pl.BlockSpec((blk, KPAD), lambda i: (i, 0)),
        ],
        out_shape=[
            jax.ShapeDtypeStruct((rows, d), BF16),
            jax.ShapeDtypeStruct((rows, QPAD), BF16),
            jax.ShapeDtypeStruct((rows, KPAD), BF16),
        ],
        compiler_params=params(),
        cost_estimate=cost(2 * rows * d * 800, rows * d * 6 + d * 1600),
        name="front",
    )(x, w, gain)


def make_cap(s_ref, dq_ref, dk_ref, cap_ref, nblk, own):
    dq = dq_ref[...]
    for i in range(nblk):
        rows = pl.ds(i * own, own)
        key = lax.broadcasted_iota(jnp.int32, (own, own), 0)
        query = lax.broadcasted_iota(jnp.int32, (own, own), 1) + s_ref[1 + i]
        ok = (dk_ref[rows, :] == dq) & (key <= query)
        cap_ref[rows, :] = jnp.where(ok, BIG, NEG)


def stacked(x):
    lane = lax.broadcasted_iota(jnp.int32, x.shape, 1)
    zero = jnp.zeros_like(x)
    return jnp.concatenate(
        [jnp.where(lane < DH, x, zero), jnp.where(lane >= DH, x, zero)], axis=0
    )


def unstacked(xt, own):
    pair = jnp.concatenate([xt[:DH, :own], xt[DH:, own:]], axis=0)
    return pair.T


def key_parts(kvf_ref, pair):
    ek = head_spread(pair, 0, RK, (128, RK * 128))
    ev = head_spread(pair, KCOLS - 128, RK, (128, RK * 128))
    ke = mm(kvf_ref[:, :128], ek)
    ve = mm(kvf_ref[:, 128:256], ev)
    return ke, ve


def tile_keys(kvf_ref, bk_ref, bv_ref):
    bk_ref[...] = mm(kvf_ref[:, :256], rank_tile(KA, (256, RK * 128)))
    bv_ref[...] = mm(kvf_ref[:, 128:384], rank_tile(KCOLS + KA - 128, (256, RK * 128)))


def attend_kernel(
    nblk, s_ref, qf_ref, kvg_ref, dq_ref, dk_ref, x_ref, wo_ref, g_ref,
    att_ref, q_ref, k_ref, v_ref, lse_ref, hm_ref, n_ref, kvw_ref,
    bq_ref, bk_ref, bv_ref, cap_ref, full_ref,
):
    pair = pl.program_id(0)
    own = qf_ref.shape[0]

    @pl.when(pair == 0)
    def _():
        for i in range(nblk):
            kvw_ref[pl.ds(i * own, own), :] = kvg_ref[s_ref[1 + nblk + i]]
        bq_ref[...] = mm(qf_ref[...], rank_tile(QA, (QPAD, RQ * 128)))
        tile_keys(kvw_ref, bk_ref, bv_ref)
        make_cap(s_ref, dq_ref, dk_ref, cap_ref, nblk, own)

    qe = mm(qf_ref[:, :128], head_spread(pair, 0, RQ, (128, RQ * 128)))
    qsum = qe[:, :128] * bq_ref[:, :128]
    for r in range(1, RQ):
        cols = slice(r * 128, (r + 1) * 128)
        qsum = qsum + qe[:, cols] * bq_ref[:, cols]
    q = (qsum * (1.0 / RQ)).astype(BF16)
    ke, ve = key_parts(kvw_ref, pair)
    k = ((ke[:, :128] * bk_ref[:, :128] + ke[:, 128:] * bk_ref[:, 128:]) * (1.0 / RK)).astype(BF16)
    v = ((ve[:, :128] * bv_ref[:, :128] + ve[:, 128:] * bv_ref[:, 128:]) * (1.0 / RK)).astype(BF16)
    q = q * jnp.asarray(DH ** (-0.5), BF16)
    q_ref[...] = q
    k_ref[...] = k
    v_ref[...] = v
    cap = cap_ref[...]
    st = jnp.minimum(mm(k, stacked(q), NT), jnp.concatenate([cap, cap], axis=1))
    top = jnp.max(st, axis=0, keepdims=True)
    e = jnp.exp(st - top)
    total = jnp.sum(e, axis=0, keepdims=True)
    p = (e * (1.0 / total)).astype(BF16)
    lse_ref[0] = top + jnp.log(total)
    att = unstacked(mm(v, p, TN), own).astype(BF16)
    att_ref[...] = att
    full_ref[pair] = att

    @pl.when(pair == pl.num_programs(0) - 1)
    def _():
        hm = x_ref[...].astype(F32)
        att_all = jnp.concatenate([full_ref[i] for i in range(PAIRS)], axis=1)
        hm = hm + mm(att_all, wo_ref[...])
        hm_ref[...] = hm
        r = lax.rsqrt(jnp.mean(hm * hm, axis=-1, keepdims=True) + EPS)
        n_ref[...] = (hm * r * g_ref[...]).astype(BF16)


def attend(nblk, scalars, qf, kvg, dq, dk, x, wo, gain):
    own, d = x.shape
    win = nblk * own
    whole = lambda a: pl.BlockSpec(a.shape, lambda p, a=a: (0,) * a.ndim)
    col = lambda rows: pl.BlockSpec((rows, 128), lambda p: (0, p))
    return pl.pallas_call(
        functools.partial(attend_kernel, nblk),
        grid=(PAIRS,),
        in_specs=[pl.BlockSpec(memory_space=pltpu.SMEM)]
        + [whole(a) for a in (qf, kvg, dq, dk, x, wo, gain)],
        out_specs=[
            col(own), col(own), col(win), col(win),
            pl.BlockSpec((1, 1, 2 * own), lambda p: (p, 0, 0)),
            pl.BlockSpec((own, d), lambda p: (0, 0)),
            pl.BlockSpec((own, d), lambda p: (0, 0)),
            pl.BlockSpec((win, KPAD), lambda p: (0, 0)),
        ],
        out_shape=[
            jax.ShapeDtypeStruct((own, d), BF16),
            jax.ShapeDtypeStruct((own, d), BF16),
            jax.ShapeDtypeStruct((win, d), BF16),
            jax.ShapeDtypeStruct((win, d), BF16),
            jax.ShapeDtypeStruct((PAIRS, 1, 2 * own), F32),
            jax.ShapeDtypeStruct((own, d), F32),
            jax.ShapeDtypeStruct((own, d), BF16),
            jax.ShapeDtypeStruct((win, KPAD), BF16),
        ],
        scratch_shapes=[
            pltpu.VMEM((own, RQ * 128), F32),
            pltpu.VMEM((win, RK * 128), F32),
            pltpu.VMEM((win, RK * 128), F32),
            pltpu.VMEM((win, own), F32),
            pltpu.VMEM((PAIRS, own, 128), BF16),
        ],
        compiler_params=params(),
        cost_estimate=cost(12e9, 12e6),
        name="attend",
    )(scalars, qf, kvg, dq, dk, x, wo, gain)


def ffn_kernel(has_prev, bf16_out, *refs):
    if has_prev:
        n_ref, c_ref, wg_ref, wu_ref, wd_ref, pg_ref, pu_ref, pd_ref = refs[:8]
        refs = refs[8:]
    else:
        n_ref, c_ref, wg_ref, wu_ref, wd_ref = refs[:5]
        refs = refs[5:]
    o_ref, dn_ref, og_ref, ou_ref, od_ref = refs[:5]
    if bf16_out:
        ag_ref, au_ref, ad_ref = refs[5:]
    else:
        ag_ref, au_ref, ad_ref = og_ref, ou_ref, od_ref
    step = pl.program_id(0)

    @pl.when(step == 0)
    def _():
        if has_prev:
            ag_ref[...] = pg_ref[...]
            au_ref[...] = pu_ref[...]
            ad_ref[...] = pd_ref[...]
        else:
            ag_ref[...] = jnp.zeros_like(ag_ref)
            au_ref[...] = jnp.zeros_like(au_ref)
            ad_ref[...] = jnp.zeros_like(ad_ref)

    n = n_ref[0]
    c = c_ref[0]
    wg, wu, wd = wg_ref[...], wu_ref[...], wd_ref[...]
    g = mm(n, wg)
    u = mm(n, wu)
    dh = mm(c, wd, NT)
    s = 1.0 / (1.0 + jnp.exp(-g))
    gs = g * s
    hid = (gs * u).astype(BF16)
    dg = (dh * u * (s * (1.0 + g * (1.0 - s)))).astype(BF16)
    du = (dh * gs).astype(BF16)
    o_ref[0] = mm(hid, wd).astype(BF16)
    dn_ref[0] = (mm(dg, wg, NT) + mm(du, wu, NT)).astype(BF16)
    ag_ref[...] += mm(n, dg, TN)
    au_ref[...] += mm(n, du, TN)
    ad_ref[...] += mm(hid, c, TN)
    if bf16_out:

        @pl.when(step == pl.num_programs(0) - 1)
        def _():
            og_ref[...] = ag_ref[...].astype(BF16)
            ou_ref[...] = au_ref[...].astype(BF16)
            od_ref[...] = ad_ref[...].astype(BF16)


def ffn(n, c, wg, wu, wd, prev, last):
    w, own, d = n.shape
    ff = wg.shape[1]
    one = lambda a: pl.BlockSpec(
        a.shape, lambda i, a=a: (0,) * a.ndim, pipeline_mode=pl.Buffered(1)
    )
    blk = pl.BlockSpec((1, own, d), lambda i: (i, 0, 0))
    dt = BF16 if last else F32
    args = [n, c, wg, wu, wd] + list(prev or [])
    shapes = [(d, ff), (d, ff), (ff, d)]
    return pl.pallas_call(
        functools.partial(ffn_kernel, bool(prev), last),
        grid=(w,),
        in_specs=[blk, blk] + [one(a) for a in args[2:]],
        out_specs=[blk, blk] + [
            pl.BlockSpec(s, lambda i: (0, 0), pipeline_mode=pl.Buffered(1)) for s in shapes
        ],
        out_shape=[jax.ShapeDtypeStruct(n.shape, BF16)] * 2
        + [jax.ShapeDtypeStruct(s, dt) for s in shapes],
        scratch_shapes=[pltpu.VMEM(s, F32) for s in shapes] if last else [],
        compiler_params=params(),
        cost_estimate=cost(18 * w * own * d * ff, 20 * w * own * d),
        name="ffn",
    )(*args)


def back_kernel(
    nblk, s_ref, q_ref, k_ref, v_ref, lse_ref, dq_ref, dk_ref, qf_ref, kvw_ref,
    dn_ref, hm_ref, c_ref, wo_ref, g_ref,
    dm_ref, dl_ref, gain_ref, gq_ref, gkv_ref,
    bq_ref, bk_ref, bv_ref, cap_ref, da_ref, aq_ref, ak_ref, av_ref, tq_ref, tk_ref, tv_ref,
):
    pair = pl.program_id(0)
    own = q_ref.shape[0]
    last = pl.num_programs(0) - 1

    @pl.when(pair == 0)
    def _():
        hm = hm_ref[...]
        dn = dn_ref[...].astype(F32)
        r = lax.rsqrt(jnp.mean(hm * hm, axis=-1, keepdims=True) + EPS)
        z = dn * g_ref[...]
        gain_ref[...] = jnp.sum(dn * hm * r, axis=0, keepdims=True)
        dm = (
            c_ref[...].astype(F32)
            + r * z
            - hm * (r * r * r) * jnp.mean(z * hm, axis=-1, keepdims=True)
        )
        dm_ref[...] = dm
        low = dm.astype(BF16)
        dl_ref[...] = low
        da = mm(low, wo_ref[...], NT).astype(BF16)
        for i in range(PAIRS):
            da_ref[i] = da[:, i * 128:(i + 1) * 128]
        bq_ref[...] = mm(qf_ref[...], rank_tile(QA, (QPAD, RQ * 128)))
        tile_keys(kvw_ref, bk_ref, bv_ref)
        make_cap(s_ref, dq_ref, dk_ref, cap_ref, nblk, own)
        for ref in (aq_ref, ak_ref, av_ref, tq_ref, tk_ref, tv_ref):
            ref[...] = jnp.zeros_like(ref)

    q = q_ref[...]
    k = k_ref[...]
    v = v_ref[...]
    qs = stacked(q)
    ds_ = stacked(da_ref[pair])
    cap = cap_ref[...]
    st = jnp.minimum(mm(k, qs, NT), jnp.concatenate([cap, cap], axis=1))
    p = jnp.exp(st - lse_ref[0])
    dp = mm(v, ds_, NT)
    delta = jnp.sum(p * dp, axis=0, keepdims=True)
    ds = (p * (dp - delta)).astype(BF16)
    dv = mm(p.astype(BF16), ds_)
    dk = mm(ds, qs)
    dq = unstacked(mm(k, ds, TN), own) * (DH ** (-0.5))

    eq = head_spread(pair, 0, RQ, (128, RQ * 128))
    qe = mm(qf_ref[:, :128], eq)
    dq6 = jnp.concatenate([dq] * RQ, axis=1)
    tq_ref[...] += dq6 * qe
    aq_ref[...] += mm((dq6 * bq_ref[...]).astype(BF16), eq, NT)
    ek = head_spread(pair, 0, RK, (128, RK * 128))
    ev = head_spread(pair, KCOLS - 128, RK, (128, RK * 128))
    ke = mm(kvw_ref[:, :128], ek)
    ve = mm(kvw_ref[:, 128:256], ev)
    dk2 = jnp.concatenate([dk] * RK, axis=1)
    dv2 = jnp.concatenate([dv] * RK, axis=1)
    tk_ref[...] += dk2 * ke
    tv_ref[...] += dv2 * ve
    ak_ref[...] += mm((dk2 * bk_ref[...]).astype(BF16), ek, NT)
    av_ref[...] += mm((dv2 * bv_ref[...]).astype(BF16), ev, NT)

    @pl.when(pair == last)
    def _():
        def fold(x, t):
            hi = x.astype(BF16)
            lo = (x - hi.astype(F32)).astype(BF16)
            return mm(hi, t, NT) + mm(lo, t, NT)

        gq = fold(tq_ref[...], rank_tile(QA, (QPAD, RQ * 128)))
        gq_ref[:, :128] = ((gq[:, :128] + aq_ref[...]) * (1.0 / RQ)).astype(BF16)
        gq_ref[:, 128:] = (gq[:, 128:] * (1.0 / RQ)).astype(BF16)
        gk = fold(tk_ref[...], rank_tile(KA, (KPAD, RK * 128)))
        gv = fold(tv_ref[...], rank_tile(KCOLS + KA, (KPAD, RK * 128)))
        gkv = gk + gv
        first = ((gkv[:, :128] + ak_ref[...]) * (1.0 / RK)).astype(BF16)
        second = ((gkv[:, 128:256] + av_ref[...]) * (1.0 / RK)).astype(BF16)
        third = (gkv[:, 256:] * (1.0 / RK)).astype(BF16)
        gkv_ref[...] = jnp.zeros_like(gkv_ref)
        for i in range(nblk):
            rows = slice(i * own, (i + 1) * own)
            slot = s_ref[1 + nblk + i]
            gkv_ref[slot, :, :128] = first[rows]
            gkv_ref[slot, :, 128:256] = second[rows]
            gkv_ref[slot, :, 256:] = third[rows]


def back(nblk, width, scalars, q, k, v, lse, dq, dk, qf, kvw, dn, hm, c, wo, gain):
    own, d = q.shape
    win = nblk * own
    whole = lambda a: pl.BlockSpec(a.shape, lambda p, a=a: (0,) * a.ndim)
    col = lambda rows: pl.BlockSpec((rows, 128), lambda p: (0, p))
    fixed = lambda *s: pl.BlockSpec(s, lambda p: (0,) * len(s))
    return pl.pallas_call(
        functools.partial(back_kernel, nblk),
        grid=(PAIRS,),
        in_specs=[
            pl.BlockSpec(memory_space=pltpu.SMEM), col(own), col(win), col(win),
            pl.BlockSpec((1, 1, 2 * own), lambda p: (p, 0, 0)),
        ] + [whole(a) for a in (dq, dk, qf, kvw, dn, hm, c, wo, gain)],
        out_specs=[
            fixed(own, d), fixed(own, d), fixed(1, d), fixed(own, QPAD),
            fixed(width, own, KPAD),
        ],
        out_shape=[
            jax.ShapeDtypeStruct((own, d), F32),
            jax.ShapeDtypeStruct((own, d), BF16),
            jax.ShapeDtypeStruct((1, d), F32),
            jax.ShapeDtypeStruct((own, QPAD), BF16),
            jax.ShapeDtypeStruct((width, own, KPAD), BF16),
        ],
        scratch_shapes=[
            pltpu.VMEM((own, RQ * 128), F32),
            pltpu.VMEM((win, RK * 128), F32),
            pltpu.VMEM((win, RK * 128), F32),
            pltpu.VMEM((win, own), F32),
            pltpu.VMEM((PAIRS, own, 128), BF16),
            pltpu.VMEM((own, 128), F32),
            pltpu.VMEM((win, 128), F32),
            pltpu.VMEM((win, 128), F32),
            pltpu.VMEM((own, RQ * 128), F32),
            pltpu.VMEM((win, RK * 128), F32),
            pltpu.VMEM((win, RK * 128), F32),
        ],
        compiler_params=params(),
        cost_estimate=cost(30e9, 15e6),
        name="back",
    )(scalars, q, k, v, lse, dq, dk, qf, kvw, dn, hm, c, wo, gain)


def swap(x, axis, size, bit):
    return lax.ppermute(x, axis, [(i, i ^ bit) for i in range(size)])


def steps_of(size):
    bits, b = [], size // 2
    while b:
        bits.append(b)
        b //= 2
    return bits


def gather(x, size):
    buf = x[None]
    for bit in steps_of(size):
        buf = jnp.concatenate([buf, swap(buf, "wide", size, bit)], axis=0)
    return buf


def order_of(size):
    order = [0]
    for bit in steps_of(size):
        order = order + [o ^ bit for o in order]
    return order


def scatter(parts, size):
    for bit in reversed(steps_of(size)):
        half = parts.shape[0] // 2
        got = swap(parts[half:], "wide", size, bit)
        total = parts[:half].astype(F32) + got.astype(F32)
        parts = total if half == 1 else total.astype(BF16)
    return parts[0]


def body(
    tokens, doc_ids, factor_weight, output_weight, norm_one, norm_two,
    gate_weight, up_weight, down_weight, cotangent,
):
    seqs, own, d = tokens.shape
    full_len = doc_ids.shape[1]
    size = full_len // own
    me = lax.axis_index("wide")
    left = min(-(-(MAX_DOC - 1) // own), size - 1)
    nblk = left + 1
    start = jnp.maximum(me - left, 0)
    order = order_of(size)
    slot_of = [order.index(j) for j in range(size)]
    slots = jnp.asarray(slot_of, jnp.int32)
    blocks = start + jnp.arange(nblk, dtype=jnp.int32)
    scalars = jnp.concatenate(
        [me[None].astype(jnp.int32), (me - blocks) * own, slots[me ^ blocks]]
    ).astype(jnp.int32)
    g1 = norm_one[None]
    g2 = norm_two[None]

    n1, qf, kvf = front(tokens.reshape(seqs * own, d), factor_weight, g1)
    qf = qf.reshape(seqs, own, QPAD)
    kvg = gather(kvf.reshape(seqs, own, KPAD), size)
    doc_query = lax.dynamic_slice_in_dim(doc_ids, me * own, own, 1)
    doc_key = lax.dynamic_slice_in_dim(doc_ids, start * own, nblk * own, 1)
    cots = [gather(cotangent[s], size) for s in range(seqs)]

    fwd = []
    for s in range(seqs):
        dq = doc_query[s][None, :]
        dk = doc_key[s][:, None]
        fwd.append(
            (dq, dk)
            + tuple(attend(nblk, scalars, qf[s], kvg[:, s], dq, dk, tokens[s], output_weight, g2))
        )
    prev = None
    outs, dns = [], []
    for s in range(seqs):
        n2 = gather(fwd[s][8], size)
        res = ffn(n2, cots[s], gate_weight, up_weight, down_weight, prev, s == seqs - 1)
        outs.append(res[0])
        dns.append(res[1])
        prev = res[2:]
    grads = [lax.psum(g, "rows").astype(F32) for g in prev]

    output, mids, lows, gain_two, gqs, gkvs = [], [], [], 0.0, [], []
    for s in range(seqs):
        dq, dk, att, q, k, v, lse, hm, n2, kvw = fwd[s]
        dn = scatter(dns[s], size)
        dm, low, gain, gq, gkv = back(
            nblk, size, scalars, q, k, v, lse, dq, dk, qf[s], kvw, dn, hm,
            cotangent[s], output_weight, g2,
        )
        output.append((hm + scatter(outs[s], size)).astype(BF16))
        mids.append(dm)
        lows.append(low)
        gqs.append(gq)
        gkvs.append(gkv)
        gain_two = gain_two + gain
    att_all = jnp.stack([f[2] for f in fwd]).reshape(seqs * own, d)
    grad_out = mm(att_all, jnp.stack(lows).reshape(seqs * own, d), TN)
    gkv = scatter(jnp.stack(gkvs, axis=1), size).astype(BF16)
    dfac = jnp.concatenate([jnp.stack(gqs)[..., :QCOLS], gkv[..., :KV]], axis=-1)
    dfac = dfac.reshape(seqs * own, -1)
    grad_factors = mm(n1, dfac, TN)
    dn1 = mm(dfac, factor_weight, NT)
    hin = tokens.reshape(seqs * own, d).astype(F32)
    r1 = lax.rsqrt(jnp.mean(hin * hin, axis=-1, keepdims=True) + EPS)
    z1 = dn1 * g1
    gain_one = jnp.sum(dn1 * hin * r1, axis=0)
    grad_norm = r1 * z1 - hin * (r1 * r1 * r1) * jnp.mean(z1 * hin, axis=-1, keepdims=True)
    input_grad = (jnp.stack(mids).reshape(seqs * own, d) + grad_norm).astype(BF16)
    packed = jnp.concatenate(
        [grad_out, jnp.pad(grad_factors.T, ((0, 0), (0, 0))), gain_one[None], gain_two], axis=0
    )
    packed = lax.psum(packed.astype(BF16), ("rows", "wide")).astype(F32)
    fac = grad_factors.shape[1]
    return (
        jnp.stack(output),
        input_grad.reshape(seqs, own, d),
        packed[d:d + fac].T,
        packed[:d],
        packed[d + fac],
        packed[d + fac + 1],
        grads[0],
        grads[1],
        grads[2],
    )


def solution(mesh):
    placed = (
        P("rows", "wide", None), P("rows", None), P(), P(), P(), P(),
        P(None, "wide"), P(None, "wide"), P("wide", None), P("rows", "wide", None),
    )
    return jax.shard_map(
        body,
        mesh=mesh,
        in_specs=placed,
        out_specs=(
            P("rows", "wide", None), P("rows", "wide", None), P(), P(), P(), P(),
            P(None, "wide"), P(None, "wide"), P("wide", None),
        ),
        check_vma=False,
    )
```

time: 904 us -> 506 us (0.56)
  matrix products: 259 us -> 7.64 us
  waiting for transfers between devices: 411 us -> 220 us
  Pallas kernels: 0 us -> 135 us
  local copies, waits for them, and re-layouts: 102 us -> 57.7 us
  blocking collectives: 40.9 us -> 0 us
  other arithmetic: 71.4 us -> 45 us
  starting transfers between devices: 0.54 us -> 17 us
    dot_general x31 -> x3, matrix products: 259 us -> 7.64 us  [mm(): return lax.dot_general(a, b, dims, preferred_element_type=F32)]
    pallas_call x0 -> x7, Pallas kernels: none -> 135 us  [the longest x2 52.2 us: back(): pl.pallas_call(functools.partial(back_kernel, nblk), grid=(PAIRS,), in_sp...]
    psum x2, waiting for transfers between devices: 253 us -> 164 us  [the longest x1 137 us: body(): packed = lax.psum(packed.astype(BF16), ('rows', 'wide')).astype(F32)]
    reduce_scatter x3 -> x0, waiting for transfers between devices: 80.4 us -> none  [the longest x1 43.8 us: body(): lax.psum_scatter(partial_output.astype(jnp.bfloat16), 'wide', scatter_dim...]
    all_gather x3 -> x0, waiting for transfers between devices: 76.8 us -> none  [the longest x1 33.8 us: body(): lax.all_gather(second_normalized, 'wide', axis=1, tiled=True)]
    ppermute x0 -> x20, waiting for transfers between devices: none -> 55.9 us  [swap(): return lax.ppermute(x, axis, [(i, i ^ bit) for i in range(size)])]
    psum x1 -> x0, blocking collectives: 40.9 us -> none  [body(): lax.psum((grad_w_factors, grad_w_out, gain_one, gain_two), ('rows', 'wide'))]
    dot_general x8 -> x0, local copies, waits for them, and re-layouts: 40.4 us -> none  [the longest x3 31 us: expand(): jnp.einsum('...hr,...rd->...hd', left_part, right_part, preferred_element...]
  transfers between devices with their start and end apart: 8 -> 22, of which waited for: 7 -> 8; matrix products, arithmetic and copies ran while one was open for 12% -> 19% of each run, Pallas kernels for 0% -> 26%
where the time goes in v1:
time: 506 us; the launch traced here: 497 us
  waiting for transfers between devices  220 us (43%)
  Pallas kernels  135 us (27%)
  local copies, waits for them, and re-layouts  57.7 us (11%)
  other arithmetic  45 us (9%)
  starting transfers between devices  17 us (3%)
  between operations  14.9 us (3%)
  matrix products  7.64 us (2%)
    psum x1, waiting for transfers between devices, body(): packed = lax.psum(packed.astype(BF16), ('rows', 'wide')).astype(F32)  137 us
    ppermute x20, waiting for transfers between devices, swap(): return lax.ppermute(x, axis, [(i, i ^ bit) for i in range(size)])  55.9 us
    pallas_call x2, Pallas kernels, back(): pl.pallas_call(functools.partial(back_kernel, nblk), grid=(PAIRS,), in_sp...  52.2 us
    pallas_call x2, Pallas kernels, ffn(): pl.pallas_call(functools.partial(ffn_kernel, bool(prev), last), grid=(w,)...  46.3 us
    pallas_call x2, Pallas kernels, attend(): pl.pallas_call(functools.partial(attend_kernel, nblk), grid=(PAIRS,), in_...  32.3 us
    psum x1, waiting for transfers between devices, body(): grads = [lax.psum(g, 'rows').astype(F32) for g in prev]  26.7 us
    concatenate x10, other arithmetic, gather(): buf = jnp.concatenate([buf, swap(buf, 'wide', size, bit)], axis=0)  21.1 us
    concatenate x1, local copies, waits for them, and re-layouts, body(): jnp.concatenate([grad_out, jnp.pad(grad_factors.T, ((0, 0), (0, 0))), gai...  18 us
  transfers between devices with their start and end apart: 22, of which 8 were waited for; matrix products, arithmetic and copies ran while one was open for 19% of the time, Pallas kernels for 26%

profile of v1, /device:TPU:0, one launch (start us, length us, event | category | flops | bytes accessed | tf_op | source)
XLA Modules:
  0.0 497.3 jit_solution(11494215483225975115)
XLA Ops:
  7.2 3.7 copy.28.w_ref
  10.9 4.2 front.1
  15.2 3.0 collective-permute-start
  22.4 6.2 %collective-permute-done = bf16[1,2,256,384]{3,2,0,1:T(8,128)(2,1)} collective-permute-done((bf16[1,2,256,384]{3,2,0,1:T(8,128)(2,1)}, bf16[1,2,256,384]{3,2,0,1:T(8,128)(2,1)}, u32[]{:S(2)}, u32[]{:S(2)}) %collective-permute-start) | collective-permute-done | bytes 393248 | tf_op jit(solution)/shard_map/ppermute | solution.py:447
  40.9 16.2 %attend.2 = (bf16[256,1024]{1,0:T(8,128)(2,1)}, bf16[256,1024]{1,0:T(8,128)(2,1)}, bf16[768,1024]{1,0:T(8,128)(2,1)}, bf16[768,1024]{1,0:T(8,128)(2,1)}, f32[8,1...) custom-call(s32[7]{0:T(128)} %pad_add_fusion.s_ref, ...), custom_call_target="tpu_custom_call" | custom-call | flops 12000000000 | bytes 12000000 | tf_op jit(solution)/shard_map/attend/pallas_call | solution.py:202
  62.8 9.3 %collective-permute-done.2 = bf16[1,256,1024]{2,1,0:T(8,128)(2,1)} collective-permute-done((bf16[1,256,1024]{2,1,0:T(8,128)(2,1)}, bf16[1,256,1024]{2,1,0:T(8,128)(2,1)}, u32[]{:S(2)}, u32[]{:S(2)}) %collective-permute-start.2) | collective-permute-done | bytes 524320 | tf_op jit(solution)/shard_map/ppermute | solution.py:447
  74.2 16.2 %attend.3 = (bf16[256,1024]{1,0:T(8,128)(2,1)}, bf16[256,1024]{1,0:T(8,128)(2,1)}, bf16[768,1024]{1,0:T(8,128)(2,1)}, bf16[768,1024]{1,0:T(8,128)(2,1)}, f32[8,1...) custom-call(s32[7]{0:T(128)} %pad_add_fusion.s_ref, ...), custom_call_target="tpu_custom_call" | custom-call | flops 12000000000 | bytes 12000000 | tf_op jit(solution)/shard_map/attend/pallas_call | solution.py:202
  100.1 2.8 pad_maximum_fusion.3.refs_1_
  107.2 2.9 pad_maximum_fusion.refs_0_
  110.1 22.1 %ffn.2 = (bf16[4,256,1024]{2,1,0:T(8,128)(2,1)}, bf16[4,256,1024]{2,1,0:T(8,128)(2,1)}, f32[1024,704]{1,0:T(8,128)}, f32[1024,704]{1,0:T(8,128)}, f32[704,1024]{1,0:T(8,128)}) custom-call(bf16[4,256,1024]{2,1,0:T(8,128)(2,1)} %pad_maximum_fusion.refs_0_, bf16[4,256,1024]{2,1,0:T(8,128)(2,1)} %pad_maximum_fusion.1.refs_1_, bf16[1024,704]{1,0:T(8,128)(2,1)} %copy.30.refs_2_, ...), custom_call_target="tpu_custom_call" | custom-call | flops 13287555072 | bytes 20971520 | tf_op jit(solution)/shard_map/ffn/pallas_call | solution.py:297
  134.0 2.9 pad_maximum_fusion.2.refs_0_
  136.9 24.2 %ffn.3 = (bf16[4,256,1024]{2,1,0:T(8,128)(2,1)}, bf16[4,256,1024]{2,1,0:T(8,128)(2,1)}, bf16[1024,704]{1,0:T(8,128)(2,1)}, bf16[1024,704]{1,0:T(8,128)(2,1)}, bf16[704,1024]{1,0:T(8,128)(2,1)}) custom-call(bf16[4,256,1024]{2,1,0:T(8,128)(2,1)} %pad_maximum_fusion.2.refs_0_, bf16[4,256,1024]{2,1,0:T(8,128)(2,1)} %pad_maximum_fusion.3.refs_1_, ...), custom_call_target="tpu_custom_call" | custom-call | flops 13287555072 | bytes 20971520 | tf_op jit(solution)/shard_map/ffn/pallas_call | solution.py:297
  170.4 9.6 %collective-permute-done.15 = bf16[1,256,1024]{2,1,0:T(8,128)(2,1)} collective-permute-done((bf16[1,256,1024]{2,1,0:T(8,128)(2,1)}, bf16[1,256,1024]{2,1,0:T(8,128)(2,1)}, u32[]{:S(2)}, u32[]{:S(2)}) %collective-permute-start.15) | collective-permute-done | bytes 524320 | tf_op jit(solution)/shard_map/ppermute | solution.py:447
  182.1 26.1 %back.2 = (f32[256,1024]{1,0:T(8,128)}, bf16[256,1024]{1,0:T(8,128)(2,1)}, f32[1,1024]{1,0:T(1,128)}, bf16[256,512]{1,0:T(8,128)(2,1)}, bf16[4,256,384]{2,1,0:T(8,128)(2,1)}) custom-call(s32[7]{0:T(128)} %pad_add_fusion.s_ref, bf16[256,1024]{1,0:T(8,128)(2,1)} %get-tuple-element.59.q_ref, bf16[768,1024]{1,0:T(8,128)(2,1)} %get-tuple-element.60.k_ref, ...), custom_call_target="tpu_custom_call" | custom-call | flops 30000001024 | bytes 15000000 | tf_op jit(solution)/shard_map/back/pallas_call | solution.py:409
  210.4 26.2 %back.3 = (f32[256,1024]{1,0:T(8,128)}, bf16[256,1024]{1,0:T(8,128)(2,1)}, f32[1,1024]{1,0:T(1,128)}, bf16[256,512]{1,0:T(8,128)(2,1)}, bf16[4,256,384]{2,1,0:T(8,128)(2,1)}) custom-call(s32[7]{0:T(128)} %pad_add_fusion.s_ref, bf16[256,1024]{1,0:T(8,128)(2,1)} %get-tuple-element.66.q_ref, bf16[768,1024]{1,0:T(8,128)(2,1)} %get-tuple-element.67.k_ref, ...), custom_call_target="tpu_custom_call" | custom-call | flops 30000001024 | bytes 15000000 | tf_op jit(solution)/shard_map/back/pallas_call | solution.py:409
  247.4 17.5 %collective-permute-done.19 = bf16[1,2,256,384]{3,2,0,1:T(8,128)(2,1)S(1)} collective-permute-done((bf16[1,2,256,384]{3,2,0,1:T(8,128)(2,1)S(1)}, bf16[1,2,256,384]{3,2,0,1:T(8,128)(2,1)S(1)}, u32[]{:S(2)}, u32[]{:S(2)}) %collective-permute-start.19) | collective-permute-done | bytes 393248 | tf_op jit(solution)/shard_map/ppermute | solution.py:447
  265.4 2.8 fusion.6
  270.4 18.0 %concatenate.57 = bf16[1826,1024]{1,0:T(8,128)(2,1)} concatenate(bf16[1024,1024]{1,0:T(8,128)(2,1)} %bitcast_convert_fusion, bf16[800,1024]{1,0:T(8,128)(2,1)} %convolution_convert_fusion, bf16[1,1024]{1,0:T(2,128)(2,1)S(1)} %broadcast_in_dim.27, bf16[1,1024]{1,0:T(2,128)(2,1)S(1)} %add_convert_fusion.6), dimensions={0} | concatenate | bytes 7479296 | tf_op jit(solution)/shard_map/concatenate | solution.py:554
  292.7 11.2 %collective-permute-done.13 = bf16[1,256,1024]{2,1,0:T(8,128)(2,1)S(1)} collective-permute-done((bf16[1,256,1024]{2,1,0:T(8,128)(2,1)S(1)}, bf16[1,256,1024]{2,1,0:T(8,128)(2,1)S(1)}, u32[]{:S(2)}, u32[]{:S(2)}) %collective-permute-start.13) | collective-permute-done | bytes 524320 | tf_op jit(solution)/shard_map/ppermute | solution.py:447
  308.3 26.7 %all-reduce.6.cloned.1.call-done = (bf16[1024,704]{1,0:T(8,128)(2,1)}, bf16[1024,704]{1,0:T(8,128)(2,1)}, bf16[704,1024]{1,0:T(8,128)(2,1)}) async-done(((bf16[1024,704]{1,0:T(8,128)(2,1)}, bf16[1024,704]{1,0:T(8,128)(2,1)}, bf16[704,1024]{1,0:T(8,128)(2,1)}), (bf16[1024,704]{1,0:T(8,128)(2,1)}, bf16[1024,704]{1,0:T(8,128)(2,1)}, bf16[704,1024]{1,0:T(8,128)(2,1)})) %all-reduce.6.cloned.1.call-update) | async-done | bytes 4325392 | tf_op jit(solution)/shard_map/psum | solution.py:525
  335.0 3.3 convert_element_type.144
  338.3 3.1 copy.38
  343.4 137.3 %all-reduce.4.cloned.1.call-done = bf16[1826,1024]{1,0:T(8,128)(2,1)} async-done(((bf16[1826,1024]{1,0:T(8,128)(2,1)}), bf16[1826,1024]{1,0:T(8,128)(2,1)}) %all-reduce.4.cloned.1.call-update) | async-done | bytes 3739664 | tf_op jit(solution)/shard_map/psum | solution.py:557
  480.7 2.9 convert_element_type.141
  (159 shorter events, 84.1 us)
Async XLA Ops:
  7.2 327.8 %all-reduce.6.cloned.1.call-start = ((), (), s32[]{:S(2)}) async-start(), calls=%async_computation.1 | async-start | bytes 9175040 | tf_op jit(solution)/shard_map/psum | solution.py:525
  15.2 13.3 %collective-permute-start = (bf16[1,2,256,384]{3,2,0,1:T(8,128)(2,1)}, bf16[1,2,256,384]{3,2,0,1:T(8,128)(2,1)}, u32[]{:S(2)}, u32[]{:S(2)}) collective-permute-start(bf16[1,2,256,384]{3,2,0,1:T(8,128)(2,1)} %bitcast.89), channel_id=1, source_target_pairs={{0,2},{1,3},{2,0},{3,1},{4,6},{5,7},{6,4},{7,5},{8,10},{9,11},{10,... | collective-permute-start | bytes 1179656 | tf_op jit(solution)/shard_map/ppermute | solution.py:447
  19.5 40.7 %collective-permute-start.4 = (bf16[1,256,1024]{2,1,0:T(8,128)(2,1)S(1)}, bf16[1,256,1024]{2,1,0:T(8,128)(2,1)S(1)}, u32[]{:S(2)}, u32[]{:S(2)}) collective-permute-start(bf16[1,256,1024]{2,1,0:T(8,128)(2,1)S(1)} %get-tuple-element.117), channel_id=1, source_target_pairs={{0,2},{1,3},{2,0},{3,1},{4,6},{5,7},{6,4},{7,5},{8,10},{9,11},{10,... | collective-permute-start | bytes 1572872 | tf_op jit(solution)/shard_map/ppermute | solution.py:447
  19.5 41.9 %collective-permute-start.10 = (bf16[1,256,1024]{2,1,0:T(8,128)(2,1)S(1)}, bf16[1,256,1024]{2,1,0:T(8,128)(2,1)S(1)}, u32[]{:S(2)}, u32[]{:S(2)}) collective-permute-start(bf16[1,256,1024]{2,1,0:T(8,128)(2,1)S(1)} %get-tuple-element.116), channel_id=1, source_target_pairs={{0,2},{1,3},{2,0},{3,1},{4,6},{5,7},{6,4},{7,5},{8,10},{9,11},{10,... | collective-permute-start | bytes 1572872 | tf_op jit(solution)/shard_map/ppermute | solution.py:447
  30.5 7.7 %collective-permute-start.1 = (bf16[2,2,256,384]{3,2,0,1:T(8,128)(2,1)}, bf16[2,2,256,384]{3,2,0,1:T(8,128)(2,1)}, u32[]{:S(2)}, u32[]{:S(2)}) collective-permute-start(bf16[2,2,256,384]{3,2,0,1:T(8,128)(2,1)} %pad_maximum_fusion.12), channel_id=1, source_target_pairs={{0,1},{1,0},{2,3},{3,2},{4,5},{5,4},{6,7},{7,6},{8,9},{9,8},{10,11... | collective-permute-start | bytes 2359304 | tf_op jit(solution)/shard_map/ppermute | solution.py:447
  57.1 15.0 %collective-permute-start.2 = (bf16[1,256,1024]{2,1,0:T(8,128)(2,1)}, bf16[1,256,1024]{2,1,0:T(8,128)(2,1)}, u32[]{:S(2)}, u32[]{:S(2)}) collective-permute-start(bf16[1,256,1024]{2,1,0:T(8,128)(2,1)} %bitcast.83), channel_id=1, source_target_pairs={{0,2},{1,3},{2,0},{3,1},{4,6},{5,7},{6,4},{7,5},{8,10},{9,11},{10,... | collective-permute-start | bytes 1572872 | tf_op jit(solution)/shard_map/ppermute | solution.py:447
  61.2 36.1 %collective-permute-start.5 = (bf16[2,256,1024]{2,1,0:T(8,128)(2,1)}, bf16[2,256,1024]{2,1,0:T(8,128)(2,1)}, u32[]{:S(2)}, u32[]{:S(2)}) collective-permute-start(bf16[2,256,1024]{2,1,0:T(8,128)(2,1)} %pad_maximum_fusion.7), channel_id=1, source_target_pairs={{0,1},{1,0},{2,3},{3,2},{4,5},{5,4},{6,7},{7,6},{8,9},{9,8},{10,11... | collective-permute-start | bytes 3145736 | tf_op jit(solution)/shard_map/ppermute | solution.py:447
  62.5 37.6 %collective-permute-start.11 = (bf16[2,256,1024]{2,1,0:T(8,128)(2,1)}, bf16[2,256,1024]{2,1,0:T(8,128)(2,1)}, u32[]{:S(2)}, u32[]{:S(2)}) collective-permute-start(bf16[2,256,1024]{2,1,0:T(8,128)(2,1)} %pad_maximum_fusion.9), channel_id=1, source_target_pairs={{0,1},{1,0},{2,3},{3,2},{4,5},{5,4},{6,7},{7,6},{8,9},{9,8},{10,11... | collective-permute-start | bytes 3145736 | tf_op jit(solution)/shard_map/ppermute | solution.py:447
  74.2 33.0 %collective-permute-start.3 = (bf16[2,256,1024]{2,1,0:T(8,128)(2,1)}, bf16[2,256,1024]{2,1,0:T(8,128)(2,1)}, u32[]{:S(2)}, u32[]{:S(2)}) collective-permute-start(bf16[2,256,1024]{2,1,0:T(8,128)(2,1)} %pad_maximum_fusion.6), channel_id=1, source_target_pairs={{0,1},{1,0},{2,3},{3,2},{4,5},{5,4},{6,7},{7,6},{8,9},{9,8},{10,11... | collective-permute-start | bytes 3145736 | tf_op jit(solution)/shard_map/ppermute | solution.py:447
  90.4 14.7 %collective-permute-start.8 = (bf16[1,256,1024]{2,1,0:T(8,128)(2,1)}, bf16[1,256,1024]{2,1,0:T(8,128)(2,1)}, u32[]{:S(2)}, u32[]{:S(2)}) collective-permute-start(bf16[1,256,1024]{2,1,0:T(8,128)(2,1)} %bitcast.86), channel_id=1, source_target_pairs={{0,2},{1,3},{2,0},{3,1},{4,6},{5,7},{6,4},{7,5},{8,10},{9,11},{10,... | collective-permute-start | bytes 1572872 | tf_op jit(solution)/shard_map/ppermute | solution.py:447
  107.2 26.9 %collective-permute-start.9 = (bf16[2,256,1024]{2,1,0:T(8,128)(2,1)}, bf16[2,256,1024]{2,1,0:T(8,128)(2,1)}, u32[]{:S(2)}, u32[]{:S(2)}) collective-permute-start(bf16[2,256,1024]{2,1,0:T(8,128)(2,1)} %pad_maximum_fusion.8), channel_id=1, source_target_pairs={{0,1},{1,0},{2,3},{3,2},{4,5},{5,4},{6,7},{7,6},{8,9},{9,8},{10,11... | collective-permute-start | bytes 3145736 | tf_op jit(solution)/shard_map/ppermute | solution.py:447
  133.5 30.1 %collective-permute-start.14 = (bf16[2,256,1024]{2,1,0:T(8,128)(2,1)S(1)}, bf16[2,256,1024]{2,1,0:T(8,128)(2,1)S(1)}, u32[]{:S(2)}, u32[]{:S(2)}) collective-permute-start(bf16[2,256,1024]{2,1,0:T(8,128)(2,1)S(1)} %slice.141), channel_id=1, source_target_pairs={{0,1},{1,0},{2,3},{3,2},{4,5},{5,4},{6,7},{7,6},{8,9},{9,8},{10,11... | collective-permute-start | bytes 3145736 | tf_op jit(solution)/shard_map/ppermute | solution.py:447
  163.6 4.3 collective-permute-start.16
  164.8 15.1 %collective-permute-start.15 = (bf16[1,256,1024]{2,1,0:T(8,128)(2,1)}, bf16[1,256,1024]{2,1,0:T(8,128)(2,1)}, u32[]{:S(2)}, u32[]{:S(2)}) collective-permute-start(bf16[1,256,1024]{2,1,0:T(8,128)(2,1)} %slice.167), channel_id=1, source_target_pairs={{0,2},{1,3},{2,0},{3,1},{4,6},{5,7},{6,4},{7,5},{8,10},{9,11},{10,... | collective-permute-start | bytes 1572872 | tf_op jit(solution)/shard_map/ppermute | solution.py:447
  167.6 72.2 %collective-permute-start.6 = (bf16[2,256,1024]{2,1,0:T(8,128)(2,1)}, bf16[2,256,1024]{2,1,0:T(8,128)(2,1)}, u32[]{:S(2)}, u32[]{:S(2)}) collective-permute-start(bf16[2,256,1024]{2,1,0:T(8,128)(2,1)} %slice.127), channel_id=1, source_target_pairs={{0,1},{1,0},{2,3},{3,2},{4,5},{5,4},{6,7},{7,6},{8,9},{9,8},{10,11... | collective-permute-start | bytes 3145736 | tf_op jit(solution)/shard_map/ppermute | solution.py:447
  167.9 312.8 %all-reduce.4.cloned.1.call-start = ((), (), s32[]{:S(2)}) async-start(), calls=%async_computation | async-start | bytes 7503872 | tf_op jit(solution)/shard_map/psum | solution.py:557
  169.9 38.3 %collective-permute-start.17 = (bf16[1,256,1024]{2,1,0:T(8,128)(2,1)S(1)}, bf16[1,256,1024]{2,1,0:T(8,128)(2,1)}, u32[]{:S(2)}, u32[]{:S(2)}) collective-permute-start(bf16[1,256,1024]{2,1,0:T(8,128)(2,1)S(1)} %slice.169), channel_id=1, source_target_pairs={{0,2},{1,3},{2,0},{3,1},{4,6},{5,7},{6,4},{7,5},{8,10},{9,11},{10,... | collective-permute-start | bytes 1572872 | tf_op jit(solution)/shard_map/ppermute | solution.py:447
  210.4 26.2 %copy-start.3 = (bf16[4,256,384]{2,1,0:T(8,128)(2,1)S(1)}, bf16[4,256,384]{2,1,0:T(8,128)(2,1)}, u32[]{:S(2)}) copy-start(bf16[4,256,384]{2,1,0:T(8,128)(2,1)} %get-tuple-element.75) | copy-start | bytes 2359300
  237.9 6.2 %collective-permute-start.18 = (bf16[2,2,256,384]{3,2,0,1:T(8,128)(2,1)S(1)}, bf16[2,2,256,384]{3,2,0,1:T(8,128)(2,1)S(1)}, u32[]{:S(2)}, u32[]{:S(2)}) collective-permute-start(bf16[2,2,256,384]{3,2,0,1:T(8,128)(2,1)S(1)} %pad_maximum_fusion.11), channel_id=1, source_target_pairs={{0,1},{1,0},{2,3},{3,2},{4,5},{5,4},{6,7},{7,6},{8,9},{9,8},{10,11... | collective-permute-start | bytes 2359304 | tf_op jit(solution)/shard_map/ppermute | solution.py:447
  239.3 49.1 %collective-permute-start.12 = (bf16[2,256,1024]{2,1,0:T(8,128)(2,1)}, bf16[2,256,1024]{2,1,0:T(8,128)(2,1)}, u32[]{:S(2)}, u32[]{:S(2)}) collective-permute-start(bf16[2,256,1024]{2,1,0:T(8,128)(2,1)} %slice.137), channel_id=1, source_target_pairs={{0,1},{1,0},{2,3},{3,2},{4,5},{5,4},{6,7},{7,6},{8,9},{9,8},{10,11... | collective-permute-start | bytes 3145736 | tf_op jit(solution)/shard_map/ppermute | solution.py:447
  242.3 50.1 %collective-permute-start.7 = (bf16[1,256,1024]{2,1,0:T(8,128)(2,1)}, bf16[1,256,1024]{2,1,0:T(8,128)(2,1)S(1)}, u32[]{:S(2)}, u32[]{:S(2)}) collective-permute-start(bf16[1,256,1024]{2,1,0:T(8,128)(2,1)} %slice.162), channel_id=1, source_target_pairs={{0,2},{1,3},{2,0},{3,1},{4,6},{5,7},{6,4},{7,5},{8,10},{9,11},{10,... | collective-permute-start | bytes 1572872 | tf_op jit(solution)/shard_map/ppermute | solution.py:447
  244.3 20.6 %collective-permute-start.19 = (bf16[1,2,256,384]{3,2,0,1:T(8,128)(2,1)S(1)}, bf16[1,2,256,384]{3,2,0,1:T(8,128)(2,1)S(1)}, u32[]{:S(2)}, u32[]{:S(2)}) collective-permute-start(bf16[1,2,256,384]{3,2,0,1:T(8,128)(2,1)S(1)} %slice.173), channel_id=1, source_target_pairs={{0,2},{1,3},{2,0},{3,1},{4,6},{5,7},{6,4},{7,5},{8,10},{9,11},{10,... | collective-permute-start | bytes 1179656 | tf_op jit(solution)/shard_map/ppermute | solution.py:447
  244.7 20.3 %copy-start.21 = (bf16[256,512]{1,0:T(8,128)(2,1)S(1)}, bf16[256,512]{1,0:T(8,128)(2,1)}, u32[]{:S(2)}) copy-start(bf16[256,512]{1,0:T(8,128)(2,1)} %get-tuple-element.73) | copy-start | bytes 786436
  290.6 13.3 %collective-permute-start.13 = (bf16[1,256,1024]{2,1,0:T(8,128)(2,1)S(1)}, bf16[1,256,1024]{2,1,0:T(8,128)(2,1)S(1)}, u32[]{:S(2)}, u32[]{:S(2)}) collective-permute-start(bf16[1,256,1024]{2,1,0:T(8,128)(2,1)S(1)} %slice.165), channel_id=1, source_target_pairs={{0,2},{1,3},{2,0},{3,1},{4,6},{5,7},{6,4},{7,5},{8,10},{9,11},{10,... | collective-permute-start | bytes 1572872 | tf_op jit(solution)/shard_map/ppermute | solution.py:447
  (29 other events, 214.4 us)
Sparse Core Ops, SparseCore 0:
  168.0 166.9 all-reduce.5
  341.2 139.4 all-reduce.3

commit v2 on v1

--- a/solution.py
+++ b/solution.py
@@ -441,6 +441,806 @@
         cost_estimate=cost(30e9, 15e6),
         name="back",
     )(scalars, q, k, v, lse, dq, dk, qf, kvw, dn, hm, c, wo, gain)
+
+
+def flip(index, bit):
+    digit = (index // bit) % 2
+    return index + bit - 2 * bit * digit
+
+
+AXES = {"c": ("wide", 1), "x": ("wide", 2), "y": ("rows", 1), "n": ("rows", 2), "f": ("rows", 4)}
+
+
+def enter(names):
+    barrier = pltpu.get_barrier_semaphore()
+    for name in names:
+        pl.semaphore_signal(
+            barrier, inc=1, device_id=partner(name), device_id_type=pl.DeviceIdType.MESH
+        )
+    pl.semaphore_wait(barrier, len(names))
+
+
+def partner(name):
+    axis, bit = AXES[name]
+    return {axis: flip(lax.axis_index(axis), bit)}
+
+
+def digit(name):
+    axis, bit = AXES[name]
+    return (lax.axis_index(axis) // bit) % 2
+
+
+def wide_digits(index):
+    return index // 2, index % 2
+
+
+def slot_for(me, block):
+    mx, mc = wide_digits(me)
+    bx, bc = wide_digits(block)
+    return 2 * ((mc + bc) % 2) + (mx + bx) % 2
+
+
+def send_to(name, src, dst, send, recv):
+    return pltpu.make_async_remote_copy(
+        src_ref=src, dst_ref=dst, send_sem=send, recv_sem=recv,
+        device_id=partner(name), device_id_type=pl.DeviceIdType.MESH,
+    )
+
+
+class Gather:
+    def __init__(self, ref, send, recv):
+        self.x = send_to("x", ref.at[0], ref.at[1], send.at[0], recv.at[0])
+        self.c = send_to("c", ref.at[0], ref.at[2], send.at[1], recv.at[1])
+        self.r = send_to("c", ref.at[1], ref.at[3], send.at[2], recv.at[2])
+
+    def first(self):
+        self.x.start()
+        self.c.start()
+
+    def relay(self):
+        self.x.wait()
+        self.r.start()
+
+    def done(self):
+        self.c.wait()
+        self.r.wait()
+
+
+class Scatter:
+    def __init__(self, part, got, last, send, recv):
+        self.part, self.got, self.last = part, got, last
+        self.c = send_to("c", part.at[pl.ds(2, 2)], got, send.at[0], recv.at[0])
+        if last is not None:
+            self.x = send_to("x", part.at[1], last, send.at[1], recv.at[1])
+
+    def core(self):
+        self.c.start()
+
+    def kept(self, i):
+        return self.part[i].astype(F32) + self.got[i].astype(F32)
+
+    def cross(self):
+        self.c.wait()
+        self.part[1] = self.kept(1).astype(BF16)
+        self.x.start()
+        self.part[0] = self.kept(0).astype(BF16)
+
+    def total(self):
+        self.x.wait()
+        return self.part[0].astype(F32) + self.last[...].astype(F32)
+
+
+class Sum:
+    def __init__(self, names, unit, src, base, acc, got, res, rbase, send, recv, local=None):
+        self.names, self.unit, self.n = names, unit, len(names)
+        self.src, self.base, self.acc, self.got = src, base, acc, got
+        self.res, self.rbase, self.send, self.recv = res, rbase, send, recv
+        self.local = local
+
+    def low(self, i, skip=0):
+        total = 0
+        for j in range(skip, i):
+            total = total + digit(self.names[j]) * 2 ** (self.n - 1 - j)
+        return total
+
+    def span(self, ref, base, chunk, count):
+        return ref.at[pl.ds(base + chunk * self.unit, count * self.unit)]
+
+    def keep(self):
+        half = 2 ** (self.n - 1)
+        return pltpu.make_async_copy(
+            self.span(self.src, self.base, self.low(1), half), self.acc, self.local
+        )
+
+    def halve(self, i):
+        half = 2 ** (self.n - 1 - i)
+        away = (1 - digit(self.names[i])) * half
+        if i == 0:
+            src = self.span(self.src, self.base, away, half)
+        else:
+            src = self.span(self.acc, 0, self.low(i, 1) + away, half)
+        dst = self.span(self.got, 0, 2 ** self.n - 2 * half, half)
+        return send_to(self.names[i], src, dst, self.send.at[i], self.recv.at[i])
+
+    def begin(self):
+        self.halve(0).start()
+        if self.local is not None:
+            self.keep().start()
+
+    def double(self, i):
+        half = 2 ** (self.n - 1 - i)
+        held = self.span(self.res, self.rbase, self.low(i + 1), half)
+        k = self.n + i
+        return send_to(self.names[i], held, held, self.send.at[k], self.recv.at[k])
+
+    def add(self, i):
+        half = 2 ** (self.n - 1 - i)
+        offset = (2 ** self.n - 2 * half) * self.unit
+        self.halve(i).wait()
+        kept = self.low(i + 1, 1) * self.unit
+        first = i == 0 and self.local is None
+        if i == 0 and self.local is not None:
+            self.keep().wait()
+        own = self.base + self.low(1) * self.unit
+        last = i == self.n - 1
+        place = self.rbase + self.low(self.n) * self.unit
+
+        def one(j, carry):
+            mine = self.src[own + j] if first else self.acc[kept + j]
+            value = (mine.astype(F32) + self.got[offset + j].astype(F32)).astype(BF16)
+            if last:
+                self.res[place + j] = value
+            else:
+                self.acc[kept + j] = value
+            return carry
+
+        lax.fori_loop(0, half * self.unit, one, 0)
+
+    def step(self, k):
+        n = self.n
+        if k < n:
+            self.add(k)
+            if k < n - 1:
+                self.halve(k + 1).start()
+            else:
+                self.double(n - 1).start()
+        else:
+            i = 2 * n - 1 - k
+            self.double(i).wait()
+            if i > 0:
+                self.double(i - 1).start()
+
+
+def fill_cap(me, first, dq, dk, cap_ref, nblk, own):
+    for i in range(nblk):
+        rows = pl.ds(i * own, own)
+        key = lax.broadcasted_iota(jnp.int32, (own, own), 0)
+        query = lax.broadcasted_iota(jnp.int32, (own, own), 1) + (me - first - i) * own
+        ok = (dk[i * own:(i + 1) * own, :] == dq) & (key <= query)
+        cap_ref[rows, :] = jnp.where(ok, BIG, NEG)
+
+
+def fore_kernel(
+    nblk, x_ref, wt_ref, wo_ref, g1_ref, g2_ref, dq_ref, dk_ref, c_ref,
+    n1_ref, qf_ref, kvw_ref, att_ref, q_ref, k_ref, v_ref, lse_ref, hm_ref, ng_ref, cg_ref,
+    kvg_ref, bq_ref, bk_ref, bv_ref, cap_ref, full_ref, send, recv,
+):
+    seqs, own, d = x_ref.shape
+    me = lax.axis_index("wide")
+    first = me // 3
+    kvs = [Gather(kvg_ref.at[s], send.at[s], recv.at[s]) for s in range(seqs)]
+    cots = [Gather(cg_ref.at[s], send.at[2 + s], recv.at[2 + s]) for s in range(seqs)]
+    norms = [Gather(ng_ref.at[s], send.at[4 + s], recv.at[4 + s]) for s in range(seqs)]
+    for s in range(seqs):
+        cg_ref[s, 0] = c_ref[s]
+    for s in range(seqs):
+        x = x_ref[s].astype(F32)
+        r = lax.rsqrt(jnp.mean(x * x, axis=-1, keepdims=True) + EPS)
+        n = (x * r * g1_ref[...]).astype(BF16)
+        n1_ref[s] = n
+        f = mm(n, wt_ref[...], NT).astype(BF16)
+        qf_ref[s] = f[:, :QPAD]
+        kvg_ref[s, 0, :, :KV] = f[:, QCOLS:]
+        kvg_ref[s, 0, :, KV:] = jnp.zeros((own, KPAD - KV), BF16)
+        if s == 0:
+            enter("cx")
+        kvs[s].first()
+    cots[0].first()
+    kvs[0].relay()
+    kvs[0].done()
+
+    def step(t, carry):
+        s = t // PAIRS
+        pair = t % PAIRS
+
+        @pl.when(t == PAIRS)
+        def _():
+            kvs[1].done()
+
+        @pl.when(pair == 0)
+        def _():
+            for i in range(nblk):
+                kvw_ref[s, pl.ds(i * own, own), :] = kvg_ref[s, slot_for(me, first + i)]
+            bq_ref[...] = mm(qf_ref[s], rank_tile(QA, (QPAD, RQ * 128)))
+            bk_ref[...] = mm(kvw_ref[s, :, :256], rank_tile(KA, (256, RK * 128)))
+            bv_ref[...] = mm(kvw_ref[s, :, 128:384], rank_tile(KCOLS + KA - 128, (256, RK * 128)))
+            fill_cap(me, first, dq_ref[s], dk_ref[s], cap_ref, nblk, own)
+
+        qe = mm(qf_ref[s, :, :128], head_spread(pair, 0, RQ, (128, RQ * 128)))
+        qsum = qe[:, :128] * bq_ref[:, :128]
+        for r in range(1, RQ):
+            cols = slice(r * 128, (r + 1) * 128)
+            qsum = qsum + qe[:, cols] * bq_ref[:, cols]
+        q = (qsum * (1.0 / RQ)).astype(BF16)
+        ke = mm(kvw_ref[s, :, :128], head_spread(pair, 0, RK, (128, RK * 128)))
+        ve = mm(kvw_ref[s, :, 128:256], head_spread(pair, KCOLS - 128, RK, (128, RK * 128)))
+        k = ((ke[:, :128] * bk_ref[:, :128] + ke[:, 128:] * bk_ref[:, 128:]) * (1.0 / RK)).astype(BF16)
+        v = ((ve[:, :128] * bv_ref[:, :128] + ve[:, 128:] * bv_ref[:, 128:]) * (1.0 / RK)).astype(BF16)
+        q = q * jnp.asarray(DH ** (-0.5), BF16)
+        q_ref[s, pair] = q
+        k_ref[s, pair] = k
+        v_ref[s, pair] = v
+        cap = cap_ref[...]
+        st = jnp.minimum(mm(k, stacked(q), NT), jnp.concatenate([cap, cap], axis=1))
+        top = jnp.max(st, axis=0, keepdims=True)
+        e = jnp.exp(st - top)
+        total = jnp.sum(e, axis=0, keepdims=True)
+        p = (e * (1.0 / total)).astype(BF16)
+        lse_ref[s, pair] = top + jnp.log(total)
+        full_ref[pair] = unstacked(mm(v, p, TN), own).astype(BF16)
+
+        @pl.when(pair == PAIRS - 1)
+        def _():
+            att = jnp.concatenate([full_ref[i] for i in range(PAIRS)], axis=1)
+            att_ref[s] = att
+            hm = x_ref[s].astype(F32) + mm(att, wo_ref[...])
+            hm_ref[s] = hm
+            r = lax.rsqrt(jnp.mean(hm * hm, axis=-1, keepdims=True) + EPS)
+            ng_ref[s, 0] = (hm * r * g2_ref[...]).astype(BF16)
+
+        @pl.when(t == 2)
+        def _():
+            kvs[1].relay()
+
+        @pl.when(t == 6)
+        def _():
+            cots[0].relay()
+            cots[1].first()
+
+        @pl.when(t == PAIRS - 1)
+        def _():
+            norms[0].first()
+
+        @pl.when(t == 11)
+        def _():
+            cots[1].relay()
+
+        @pl.when(t == 14)
+        def _():
+            norms[0].relay()
+
+        return carry
+
+    lax.fori_loop(0, seqs * PAIRS, step, 0)
+    norms[1].first()
+    for s in range(seqs):
+        cots[s].done()
+    norms[0].done()
+    norms[1].relay()
+    norms[1].done()
+
+
+def vmem():
+    return pl.BlockSpec(memory_space=pltpu.VMEM)
+
+
+def hbm():
+    return pl.BlockSpec(memory_space=pl.ANY)
+
+
+def fused(ident, limit=63):
+    return pltpu.CompilerParams(
+        vmem_limit_bytes=limit << 20, collective_id=ident, has_side_effects=True
+    )
+
+
+def fore(nblk, x, wt, wo, g1, g2, dq, dk, c):
+    seqs, own, d = x.shape
+    win = nblk * own
+    shape = jax.ShapeDtypeStruct
+    return pl.pallas_call(
+        functools.partial(fore_kernel, nblk),
+        in_specs=[vmem()] * 8,
+        out_specs=[vmem()] * 11,
+        out_shape=[
+            shape((seqs, own, d), BF16), shape((seqs, own, QPAD), BF16),
+            shape((seqs, win, KPAD), BF16), shape((seqs, own, d), BF16),
+            shape((seqs, PAIRS, own, 128), BF16), shape((seqs, PAIRS, win, 128), BF16),
+            shape((seqs, PAIRS, win, 128), BF16), shape((seqs, PAIRS, 1, 2 * own), F32),
+            shape((seqs, own, d), F32), shape((seqs, 4, own, d), BF16),
+            shape((seqs, 4, own, d), BF16),
+        ],
+        scratch_shapes=[
+            pltpu.VMEM((seqs, 4, own, KPAD), BF16),
+            pltpu.VMEM((own, RQ * 128), F32),
+            pltpu.VMEM((win, RK * 128), F32),
+            pltpu.VMEM((win, RK * 128), F32),
+            pltpu.VMEM((win, own), F32),
+            pltpu.VMEM((PAIRS, own, 128), BF16),
+            pltpu.SemaphoreType.DMA((6, 3)),
+            pltpu.SemaphoreType.DMA((6, 3)),
+        ],
+        compiler_params=fused(0),
+        cost_estimate=cost(30e9, 30e6),
+        name="fore",
+    )(x, wt, wo, g1, g2, dq, dk, c)
+
+
+def middle_kernel(
+    n_ref, c_ref, wg_ref, wu_ref, wd_ref,
+    dn_ref, ok_ref, os_ref, gw_ref,
+    hid_ref, dg_ref, du_ref, dp_ref, op_ref, dc_ref, dx_ref, oc_ref, send, recv,
+):
+    seqs, size, own, d = n_ref.shape
+    ff = wd_ref.shape[0]
+    downs = [
+        Scatter(dp_ref.at[s], dc_ref.at[s], dx_ref.at[s], send.at[s], recv.at[s])
+        for s in range(seqs)
+    ]
+    ups = [
+        Scatter(op_ref.at[s], oc_ref.at[s], None, send.at[seqs + s], recv.at[seqs + s])
+        for s in range(seqs)
+    ]
+    enter("cx")
+
+    def step(t, carry):
+        s = t // size
+        b = size - 1 - t % size
+        n = n_ref[s, b]
+        c = c_ref[s, b]
+        g = mm(wg_ref[...], n, NT)
+        u = mm(wu_ref[...], n, NT)
+        dh = mm(wd_ref[...], c, NT)
+        sg = 1.0 / (1.0 + jnp.exp(-g))
+        gs = g * sg
+        hid = (gs * u).astype(BF16)
+        dg = (dh * u * (sg * (1.0 + g * (1.0 - sg)))).astype(BF16)
+        du = (dh * gs).astype(BF16)
+        cols = pl.ds(pl.multiple_of((s * size + b) * own, 128), own)
+        hid_ref[:, cols] = hid
+        dg_ref[:, cols] = dg
+        du_ref[:, cols] = du
+        op_ref[s, b] = mm(hid, wd_ref[...], TN).astype(BF16)
+        dp_ref[s, b] = (mm(dg, wg_ref[...], TN) + mm(du, wu_ref[...], TN)).astype(BF16)
+        for i in range(seqs):
+
+            @pl.when(t == i * size + 1)
+            def _(i=i):
+                downs[i].core()
+                ups[i].core()
+
+            @pl.when(t == i * size + size - 1)
+            def _(i=i):
+                downs[i].cross()
+
+        return carry
+
+    lax.fori_loop(0, seqs * size, step, 0)
+    units = ff // 16
+    half = units // 2
+    rows = half * 16
+    gw_ref[pl.ds(3 * units, gw_ref.shape[0] - 3 * units)] = jnp.zeros(
+        (gw_ref.shape[0] - 3 * units, 16, d), BF16
+    )
+    for m, (a_ref, b_ref) in enumerate(((dg_ref, n_ref), (du_ref, n_ref), (hid_ref, c_ref))):
+
+        def part(i, carry, m=m, a_ref=a_ref, b_ref=b_ref):
+            a = a_ref[pl.ds(pl.multiple_of(i * rows, 16), rows), :]
+            w = mm(a, b_ref[...].reshape(seqs * size * own, d))
+            gw_ref[pl.ds(m * units + i * half, half)] = w.astype(BF16).reshape(half, 16, d)
+            return carry
+
+        lax.fori_loop(0, 2, part, 0)
+    for s in range(seqs):
+        ups[s].c.wait()
+        ok_ref[s] = ups[s].kept(0).astype(BF16)
+        os_ref[s] = ups[s].kept(1).astype(BF16)
+    for s in range(seqs):
+        dn_ref[s] = downs[s].total()
+
+
+def middle(n, c, wg, wu, wd, units):
+    seqs, size, own, d = n.shape
+    ff = wd.shape[0]
+    shape = jax.ShapeDtypeStruct
+    flat = (ff, seqs * size * own)
+    return pl.pallas_call(
+        middle_kernel,
+        in_specs=[vmem()] * 5,
+        out_specs=[vmem()] * 4,
+        out_shape=[
+            shape((seqs, own, d), F32), shape((seqs, own, d), BF16),
+            shape((seqs, own, d), BF16), shape((units, 16, d), BF16),
+        ],
+        scratch_shapes=[pltpu.VMEM(flat, BF16)] * 3
+        + [pltpu.VMEM((seqs, size, own, d), BF16)] * 2
+        + [
+            pltpu.VMEM((seqs, 2, own, d), BF16),
+            pltpu.VMEM((seqs, own, d), BF16),
+            pltpu.VMEM((seqs, 2, own, d), BF16),
+            pltpu.SemaphoreType.DMA((2 * seqs, 2)),
+            pltpu.SemaphoreType.DMA((2 * seqs, 2)),
+        ],
+        compiler_params=fused(1),
+        cost_estimate=cost(27e9, 30e6),
+        name="middle",
+    )(n, c, wg, wu, wd)
+
+
+PARTS = (("ynf", 4), ("ynf", 4), ("ynf", 4), ("nfy", 5))
+UNITS = 8 * sum(u for _, u in PARTS)
+OUT_PARTS = (("cxynf", 128), ("cxnfy", 128))
+FAC_PARTS = (("cxynf", 80), ("cynfx", 64), ("cnfxy", 64))
+FAC_ROWS = 4 * sum(r for _, r in FAC_PARTS)
+
+
+def cut(value, parts, bufs, only):
+    m = sum(r for _, r in parts)
+    at = 0
+    for g, (_, r) in enumerate(parts):
+        if g in only:
+            for i in range(32):
+                row = m * (i // 8) + at
+                bufs[g][i] = value[row:row + r, 128 * (i % 8):128 * (i % 8) + 128]
+        at += r
+
+
+def joined(results, parts):
+    cols = [r.reshape(4, 8, rows, 128) for r, (_, rows) in zip(results, parts)]
+    whole = jnp.concatenate(cols, axis=2)
+    return whole.transpose(0, 2, 1, 3).reshape(-1, 1024).astype(F32)
+
+
+def after_kernel(
+    nblk, gw_ref, dn_ref, ok_ref, os_ref, q_ref, k_ref, v_ref, lse_ref, dq_ref, dk_ref,
+    qf_ref, kvw_ref, hm_ref, c_ref, wo_ref, g1_ref, g2_ref, att_ref, n1_ref, x_ref, wt_ref,
+    out_ref, ig_ref, gr_ref, *refs,
+):
+    n_out, n_fac = len(OUT_PARTS), len(FAC_PARTS)
+    or_refs, refs = refs[:n_out], refs[n_out:]
+    fr_refs, refs = refs[:n_fac], refs[n_fac:]
+    (bq_ref, bk_ref, bv_ref, cap_ref, da_ref, aq_ref, ak_ref, av_ref, tq_ref, tk_ref, tv_ref,
+     dm_ref, late_ref, gq_ref, gkp_ref, gkc_ref, gkx_ref, ox_ref, kb_ref, vb_ref) = refs[:20]
+    refs = refs[20:]
+    gots, refs = refs[:len(PARTS)], refs[len(PARTS):]
+    accs, refs = refs[:len(PARTS)], refs[len(PARTS):]
+    ob, refs = refs[:n_out], refs[n_out:]
+    og, refs = refs[:n_out], refs[n_out:]
+    oa, refs = refs[:n_out], refs[n_out:]
+    fb, refs = refs[:n_fac], refs[n_fac:]
+    fg, refs = refs[:n_fac], refs[n_fac:]
+    fa, refs = refs[:n_fac], refs[n_fac:]
+    send, recv, loc, gs, gr, kvsem, wsem = refs
+    seqs, own, d = hm_ref.shape
+    me = lax.axis_index("wide")
+    first = me // 3
+
+    sums, base = [], 0
+    for p, (names, u) in enumerate(PARTS):
+        sums.append(Sum(
+            names, u, gw_ref, base, accs[p], gots[p], gr_ref, base, send.at[p], recv.at[p],
+            loc.at[p],
+        ))
+        base += 8 * u
+    k0 = len(PARTS)
+    outs = [
+        Sum(names, 1, ob[g], 0, oa[g], og[g], or_refs[g], 0, send.at[k0 + g], recv.at[k0 + g])
+        for g, (names, _) in enumerate(OUT_PARTS)
+    ]
+    k1 = k0 + n_out
+    facs = [
+        Sum(names, 1, fb[g], 0, fa[g], fg[g], fr_refs[g], 0, send.at[k1 + g], recv.at[k1 + g])
+        for g, (names, _) in enumerate(FAC_PARTS)
+    ]
+    keys = [
+        Scatter(gkp_ref.at[s], gkc_ref.at[s], gkx_ref.at[s], gs.at[s], gr.at[s])
+        for s in range(seqs)
+    ]
+    crosses = [
+        send_to("x", os_ref.at[s], ox_ref.at[s], gs.at[2 + s, 0], gr.at[2 + s, 0])
+        for s in range(seqs)
+    ]
+
+    def fetch(t):
+        return [
+            pltpu.make_async_copy(a.at[t // PAIRS, t % PAIRS], b.at[t % 2], kvsem.at[i, t % 2])
+            for i, (a, b) in enumerate(((k_ref, kb_ref), (v_ref, vb_ref)))
+        ]
+
+    for copy in fetch(0):
+        copy.start()
+    loads = [
+        pltpu.make_async_copy(dn_ref, dm_ref, wsem.at[0]),
+        pltpu.make_async_copy(c_ref, late_ref, wsem.at[1]),
+    ]
+    for copy in loads:
+        copy.start()
+    enter("cxynf")
+    for part in sums:
+        part.begin()
+    for cross in crosses:
+        cross.start()
+
+    for copy in loads:
+        copy.wait()
+    gain_two = jnp.zeros((1, d), F32)
+    for s in range(seqs):
+        hm = hm_ref[s]
+        dn = dm_ref[s]
+        r = lax.rsqrt(jnp.mean(hm * hm, axis=-1, keepdims=True) + EPS)
+        z = dn * g2_ref[...]
+        gain_two = gain_two + jnp.sum(dn * hm * r, axis=0, keepdims=True)
+        dm = (
+            late_ref[s].astype(F32)
+            + r * z
+            - hm * (r * r * r) * jnp.mean(z * hm, axis=-1, keepdims=True)
+        )
+        dm_ref[s] = dm
+        low = dm.astype(BF16)
+        late_ref[s] = low
+        da = mm(low, wo_ref[...], NT).astype(BF16)
+        for i in range(PAIRS):
+            da_ref[s, i] = da[:, i * 128:(i + 1) * 128]
+    go = mm(att_ref[...].reshape(seqs * own, d), late_ref[...].reshape(seqs * own, d), TN)
+    cut(go.astype(BF16), OUT_PARTS, ob, range(n_out))
+    for part in outs:
+        part.begin()
+    load_x = pltpu.make_async_copy(x_ref, late_ref, wsem.at[2])
+    load_x.start()
+
+    def finish(s):
+        def fold(x, t):
+            hi = x.astype(BF16)
+            lo = (x - hi.astype(F32)).astype(BF16)
+            return mm(hi, t, NT) + mm(lo, t, NT)
+
+        gq = fold(tq_ref[...], rank_tile(QA, (QPAD, RQ * 128)))
+        gq_ref[s, :, :128] = ((gq[:, :128] + aq_ref[...]) * (1.0 / RQ)).astype(BF16)
+        gq_ref[s, :, 128:] = (gq[:, 128:] * (1.0 / RQ)).astype(BF16)
+        gk = fold(tk_ref[...], rank_tile(KA, (KPAD, RK * 128)))
+        gv = fold(tv_ref[...], rank_tile(KCOLS + KA, (KPAD, RK * 128)))
+        gkv = gk + gv
+        one = ((gkv[:, :128] + ak_ref[...]) * (1.0 / RK)).astype(BF16)
+        two = ((gkv[:, 128:256] + av_ref[...]) * (1.0 / RK)).astype(BF16)
+        three = (gkv[:, 256:] * (1.0 / RK)).astype(BF16)
+        gkp_ref[s] = jnp.zeros_like(gkp_ref[s])
+        for i in range(nblk):
+            rows = slice(i * own, (i + 1) * own)
+            slot = slot_for(me, first + i)
+            gkp_ref[s, slot, :, :128] = one[rows]
+            gkp_ref[s, slot, :, 128:256] = two[rows]
+            gkp_ref[s, slot, :, 256:] = three[rows]
+
+    def emit(s):
+        crosses[s].wait()
+        total = hm_ref[s] + (ok_ref[s].astype(F32) + ox_ref[s].astype(F32))
+        out_ref[s] = total.astype(BF16)
+
+    events = {t: [] for t in range(2 * PAIRS)}
+    rest = []
+
+    def at(t, call):
+        (events[t] if t < 2 * PAIRS else rest).append(call)
+
+    for part, times in zip(sums, (
+        (1, 3, 5, 7, 9, 12), (4, 6, 8, 10, 12, 16), (8, 10, 12, 13, 16, 18), (1, 5, 6, 8, 11, 15),
+    )):
+        for k, t in enumerate(times):
+            at(t, functools.partial(part.step, k))
+    for g, part in enumerate(outs):
+        for k in range(10):
+            at(2 + g + k + (k // 5), functools.partial(part.step, k))
+    at(6, functools.partial(emit, 0))
+    at(8, functools.partial(emit, 1))
+    at(PAIRS + 1, keys[0].cross)
+
+    def step(t, carry):
+        s = t // PAIRS
+        pair = t % PAIRS
+        slot = t % 2
+
+        @pl.when(t < seqs * PAIRS - 1)
+        def _():
+            for copy in fetch(t + 1):
+                copy.start()
+
+        @pl.when(pair == 0)
+        def _():
+            bq_ref[...] = mm(qf_ref[s], rank_tile(QA, (QPAD, RQ * 128)))
+            bk_ref[...] = mm(kvw_ref[s, :, :256], rank_tile(KA, (256, RK * 128)))
+            bv_ref[...] = mm(kvw_ref[s, :, 128:384], rank_tile(KCOLS + KA - 128, (256, RK * 128)))
+            fill_cap(me, first, dq_ref[s], dk_ref[s], cap_ref, nblk, own)
+            for ref in (aq_ref, ak_ref, av_ref, tq_ref, tk_ref, tv_ref):
+                ref[...] = jnp.zeros_like(ref)
+
+        for copy in fetch(t):
+            copy.wait()
+        q = q_ref[s, pair]
+        k = kb_ref[slot]
+        v = vb_ref[slot]
+        qs = stacked(q)
+        da = stacked(da_ref[s, pair])
+        cap = cap_ref[...]
+        st = jnp.minimum(mm(k, qs, NT), jnp.concatenate([cap, cap], axis=1))
+        p = jnp.exp(st - lse_ref[s, pair])
+        dp = mm(v, da, NT)
+        delta = jnp.sum(p * dp, axis=0, keepdims=True)
+        ds = (p * (dp - delta)).astype(BF16)
+        dv = mm(p.astype(BF16), da)
+        dk = mm(ds, qs)
+        dq = unstacked(mm(k, ds, TN), own) * (DH ** (-0.5))
+
+        eq = head_spread(pair, 0, RQ, (128, RQ * 128))
+        qe = mm(qf_ref[s, :, :128], eq)
+        dq6 = jnp.concatenate([dq] * RQ, axis=1)
+        tq_ref[...] += dq6 * qe
+        aq_ref[...] += mm((dq6 * bq_ref[...]).astype(BF16), eq, NT)
+        ek = head_spread(pair, 0, RK, (128, RK * 128))
+        ev = head_spread(pair, KCOLS - 128, RK, (128, RK * 128))
+        ke = mm(kvw_ref[s, :, :128], ek)
+        ve = mm(kvw_ref[s, :, 128:256], ev)
+        dk2 = jnp.concatenate([dk] * RK, axis=1)
+        dv2 = jnp.concatenate([dv] * RK, axis=1)
+        tk_ref[...] += dk2 * ke
+        tv_ref[...] += dv2 * ve
+        ak_ref[...] += mm((dk2 * bk_ref[...]).astype(BF16), ek, NT)
+        av_ref[...] += mm((dv2 * bv_ref[...]).astype(BF16), ev, NT)
+
+        @pl.when(pair == PAIRS - 1)
+        def _():
+            finish(s)
+
+        @pl.when(t == PAIRS - 1)
+        def _():
+            keys[0].core()
+
+        for when, calls in events.items():
+            if calls:
+
+                @pl.when(t == when)
+                def _(calls=calls):
+                    for call in calls:
+                        call()
+
+        return carry
+
+    lax.fori_loop(0, seqs * PAIRS, step, 0)
+    keys[1].core()
+    n1 = n1_ref[...].reshape(seqs * own, d)
+    gq = gq_ref[...].reshape(seqs * own, QPAD)
+    gfq = mm(gq, n1, TN)[:QCOLS]
+    dn1 = mm(gq[:, :QCOLS], wt_ref[:QCOLS, :])
+    keys[1].cross()
+    gkv0 = keys[0].total().astype(BF16)
+    gkv = jnp.concatenate([gkv0, keys[1].total().astype(BF16)], axis=0)
+    gfk = mm(gkv, n1, TN)[:KV]
+    tail = jnp.zeros((FAC_ROWS - QCOLS - KV, d), F32)
+    gf = jnp.concatenate([gfq, gfk, tail], axis=0).astype(BF16)
+    cut(gf, FAC_PARTS, fb, range(n_fac - 1))
+    for part in facs[:-1]:
+        part.begin()
+    dn1 = dn1 + mm(gkv[:, :KV], wt_ref[QCOLS:, :])
+    load_x.wait()
+    hin = late_ref[...].reshape(seqs * own, d).astype(F32)
+    r1 = lax.rsqrt(jnp.mean(hin * hin, axis=-1, keepdims=True) + EPS)
+    z1 = dn1 * g1_ref[...]
+    gain_one = jnp.sum(dn1 * hin * r1, axis=0, keepdims=True)
+    gains = jnp.concatenate(
+        [gain_one, gain_two, jnp.zeros((FAC_ROWS - QCOLS - KV - 2, d), F32)], axis=0
+    )
+    gf = jnp.concatenate([gfq, gfk, gains], axis=0).astype(BF16)
+    cut(gf, FAC_PARTS, fb, (n_fac - 1,))
+    facs[-1].begin()
+    grad = r1 * z1 - hin * (r1 * r1 * r1) * jnp.mean(z1 * hin, axis=-1, keepdims=True)
+    ig_ref[...] = (dm_ref[...].reshape(seqs * own, d) + grad).astype(BF16).reshape(seqs, own, d)
+    tails = [functools.partial(part.step, k) for k in range(10) for part in facs]
+    while tails or rest:
+        for call in tails[:n_fac]:
+            call()
+        tails = tails[n_fac:]
+        for call in rest[:2]:
+            call()
+        rest = rest[2:]
+
+
+def after(nblk, gw, dn, ok, os, q, k, v, lse, dq, dk, qf, kvw, hm, c, wo, g1, g2, att, n1, x, wt):
+    seqs, own, d = hm.shape
+    win = nblk * own
+    shape = jax.ShapeDtypeStruct
+    far = (0, 1, 3, 5, 6, 13, 19)
+    results = [shape((32, r, 128), BF16) for _, r in OUT_PARTS + FAC_PARTS]
+    total = len(PARTS) + len(OUT_PARTS) + len(FAC_PARTS)
+    args = (gw, dn, ok, os, q, k, v, lse, dq, dk, qf, kvw, hm, c, wo, g1, g2, att, n1, x, wt)
+    res = pl.pallas_call(
+        functools.partial(after_kernel, nblk),
+        in_specs=[hbm() if i in far else vmem() for i in range(len(args))],
+        out_specs=[vmem()] * (3 + len(results)),
+        out_shape=[
+            shape((seqs, own, d), BF16), shape((seqs, own, d), BF16), shape(gw.shape, BF16),
+        ] + results,
+        scratch_shapes=[
+            pltpu.VMEM((own, RQ * 128), F32),
+            pltpu.VMEM((win, RK * 128), F32),
+            pltpu.VMEM((win, RK * 128), F32),
+            pltpu.VMEM((win, own), F32),
+            pltpu.VMEM((seqs, PAIRS, own, 128), BF16),
+            pltpu.VMEM((own, 128), F32),
+            pltpu.VMEM((win, 128), F32),
+            pltpu.VMEM((win, 128), F32),
+            pltpu.VMEM((own, RQ * 128), F32),
+            pltpu.VMEM((win, RK * 128), F32),
+            pltpu.VMEM((win, RK * 128), F32),
+            pltpu.VMEM((seqs, own, d), F32),
+            pltpu.VMEM((seqs, own, d), BF16),
+            pltpu.VMEM((seqs, own, QPAD), BF16),
+            pltpu.VMEM((seqs, 4, own, KPAD), BF16),
+            pltpu.VMEM((seqs, 2, own, KPAD), BF16),
+            pltpu.VMEM((seqs, own, KPAD), BF16),
+            pltpu.VMEM((seqs, own, d), BF16),
+            pltpu.VMEM((2, win, 128), BF16),
+            pltpu.VMEM((2, win, 128), BF16),
+        ]
+        + [pltpu.VMEM((7 * u, 16, d), BF16) for _, u in PARTS]
+        + [pltpu.VMEM((4 * u, 16, d), BF16) for _, u in PARTS]
+        + [pltpu.VMEM((n, r, 128), BF16) for n in (32, 31, 16) for _, r in OUT_PARTS]
+        + [pltpu.VMEM((n, r, 128), BF16) for n in (32, 31, 16) for _, r in FAC_PARTS]
+        + [
+            pltpu.SemaphoreType.DMA((total, 10)),
+            pltpu.SemaphoreType.DMA((total, 10)),
+            pltpu.SemaphoreType.DMA((len(PARTS),)),
+            pltpu.SemaphoreType.DMA((4, 2)),
+            pltpu.SemaphoreType.DMA((4, 2)),
+            pltpu.SemaphoreType.DMA((2, 2)),
+            pltpu.SemaphoreType.DMA((3,)),
+        ],
+        compiler_params=fused(2),
+        cost_estimate=cost(60e9, 60e6),
+        name="after",
+    )(*args)
+    n = 3 + len(OUT_PARTS)
+    return res[0], res[1], res[2], res[3:n], res[n:]
+
+
+def fused_body(
+    tokens, doc_ids, factor_weight, output_weight, norm_one, norm_two,
+    gate_weight, up_weight, down_weight, cotangent,
+):
+    seqs, own, d = tokens.shape
+    me = lax.axis_index("wide")
+    nblk = -(-(MAX_DOC - 1) // own) + 1
+    first = me // 3
+    g1 = norm_one[None]
+    g2 = norm_two[None]
+    dq = lax.dynamic_slice_in_dim(doc_ids, me * own, own, 1)[:, None, :]
+    dk = lax.dynamic_slice_in_dim(doc_ids, first * own, nblk * own, 1)[:, :, None]
+    wt = factor_weight.T
+    n1, qf, kvw, att, q, k, v, lse, hm, ng, cg = fore(
+        nblk, tokens, wt, output_weight, g1, g2, dq, dk, cotangent
+    )
+    dn, ok, os, gw = middle(ng, cg, gate_weight.T, up_weight.T, down_weight, UNITS)
+    output, input_grad, gr, go, gf = after(
+        nblk, gw, dn, ok, os, q, k, v, lse, dq, dk, qf, kvw, hm, cotangent, output_weight,
+        g1, g2, att, n1, tokens, wt,
+    )
+    ff = down_weight.shape[0]
+    gr = gr.reshape(-1, d)
+    grad_out = joined(go, OUT_PARTS)
+    fac = joined(gf, FAC_PARTS)
+    cols = factor_weight.shape[1]
+    return (
+        output, input_grad, fac[:cols].T, grad_out, fac[cols], fac[cols + 1],
+        gr[:ff].astype(F32).T, gr[ff:2 * ff].astype(F32).T, gr[2 * ff:3 * ff].astype(F32),
+    )
 
 
 def swap(x, axis, size, bit):
@@ -551,10 +1351,9 @@
     gain_one = jnp.sum(dn1 * hin * r1, axis=0)
     grad_norm = r1 * z1 - hin * (r1 * r1 * r1) * jnp.mean(z1 * hin, axis=-1, keepdims=True)
     input_grad = (jnp.stack(mids).reshape(seqs * own, d) + grad_norm).astype(BF16)
-    packed = jnp.concatenate(
-        [grad_out, jnp.pad(grad_factors.T, ((0, 0), (0, 0))), gain_one[None], gain_two], axis=0
-    )
-    packed = lax.psum(packed.astype(BF16), ("rows", "wide")).astype(F32)
+    parts = [grad_out, grad_factors.T, gain_one[None], gain_two]
+    packed = jnp.concatenate([p.astype(BF16) for p in parts], axis=0)
+    packed = lax.psum(packed, ("rows", "wide")).astype(F32)
     fac = grad_factors.shape[1]
     return (
         jnp.stack(output),
@@ -574,8 +1373,9 @@
         P("rows", "wide", None), P("rows", None), P(), P(), P(), P(),
         P(None, "wide"), P(None, "wide"), P("wide", None), P("rows", "wide", None),
     )
+    small = mesh.shape["rows"] == 8 and mesh.shape["wide"] == 4
     return jax.shard_map(
-        body,
+        fused_body if small else body,
         mesh=mesh,
         in_specs=placed,
         out_specs=(

time: 506 us -> 334 us (0.66); the launches traced: 497 us -> 333 us
  waiting for transfers between devices: 220 us -> 0 us
  Pallas kernels: 135 us -> 310 us
  local copies, waits for them, and re-layouts: 57.7 us -> 15.3 us
  other arithmetic: 45 us -> 7.63 us
  starting transfers between devices: 17 us -> 0 us
  between operations: 14.9 us -> 0.77 us
  matrix products: 7.64 us -> 0 us
    pallas_call x7 -> x3, Pallas kernels: 135 us -> 310 us  [the longest x1 189 us: after(): pl.pallas_call(functools.partial(after_kernel, nblk), in_specs=[hbm() if...]
    psum x2 -> x0, waiting for transfers between devices: 164 us -> none  [the longest x1 137 us: body(): packed = lax.psum(packed.astype(BF16), ('rows', 'wide')).astype(F32)]
    ppermute x20 -> x0, waiting for transfers between devices: 55.9 us -> none  [swap(): return lax.ppermute(x, axis, [(i, i ^ bit) for i in range(size)])]
    concatenate x12 -> x0, other arithmetic: 22.7 us -> none  [the longest x10 21.1 us: gather(): buf = jnp.concatenate([buf, swap(buf, 'wide', size, bit)], axis=0)]
    concatenate x1 -> x0, local copies, waits for them, and re-layouts: 18 us -> none  [body(): jnp.concatenate([grad_out, jnp.pad(grad_factors.T, ((0, 0), (0, 0))), gai...]
    ppermute x20 -> x0, starting transfers between devices: 16.9 us -> none  [swap(): return lax.ppermute(x, axis, [(i, i ^ bit) for i in range(size)])]
    slice x13 -> x2, local copies, waits for them, and re-layouts: 13.9 us -> 1.06 us  [the longest x1 0.6 us: fused_body(): fac[cols + 1]]
    convert_element_type x9 -> x3, other arithmetic: 14.2 us -> 4.21 us  [the longest x2 2.17 us: joined(): return whole.transpose(0, 2, 1, 3).reshape(-1, 1024).astype(F32)]
  transfers between devices with their start and end apart: 22 -> 0, of which waited for: 8 -> 0; matrix products, arithmetic and copies ran while one was open for 19% -> 0% of each run, Pallas kernels for 26% -> 0%
where the time goes in v2:
time: 334 us; the launch traced here: 333 us
  Pallas kernels  310 us (93%)
  local copies, waits for them, and re-layouts  15.3 us (5%)
  other arithmetic  7.63 us (2%)
    pallas_call x1, Pallas kernels, after(): pl.pallas_call(functools.partial(after_kernel, nblk), in_specs=[hbm() if...  189 us
    pallas_call x1, Pallas kernels, fore(): pl.pallas_call(functools.partial(fore_kernel, nblk), in_specs=[vmem()] *...  76 us
    pallas_call x1, Pallas kernels, middle(): pl.pallas_call(middle_kernel, in_specs=[vmem()] * 5, out_specs=[vmem()] *...  44.7 us
    unnamed x20, local copies, waits for them, and re-layouts  7.03 us

profile of v2, /device:TPU:0, one launch (start us, length us, event | category | flops | bytes accessed | tf_op | source)
XLA Modules:
  0.0 333.4 jit_solution(4391078978370307708)
XLA Ops:
  0.6 0.0 copy-start
  0.7 0.7 copy-done
  1.3 0.6 broadcast_in_dim.14.dq_ref
  1.9 1.2 copy.21.dk_ref
  3.1 76.0 %fore.1 = (bf16[2,256,1024]{2,1,0:T(8,128)(2,1)}, bf16[2,256,512]{2,1,0:T(8,128)(2,1)}, bf16[2,768,384]{2,1,0:T(8,128)(2,1)}, bf16[2,256,1024]{2,1,0:T(8,128)(2,...) custom-call(bf16[2,256,1024]{2,1,0:T(8,128)(2,1)} %x_ref.3, ...), custom_call_target="tpu_custom_call" | custom-call | flops 30000001024 | bytes 30000000 | tf_op jit(solution)/shard_map/fore/pallas_call | solution.py:751
  79.1 44.7 %middle.1 = (f32[2,256,1024]{2,1,0:T(8,128)}, bf16[2,256,1024]{2,1,0:T(8,128)(2,1)}, bf16[2,256,1024]{2,1,0:T(8,128)(2,1)}, bf16[136,16,1024]{2,1,0:T(8,128)(2,1)}) custom-call(bf16[2,4,256,1024]{3,2,1,0:T(8,128)(2,1)} %get-tuple-element.32.n_ref, bf16[2,4,256,1024]{3,2,1,0:T(8,128)(2,1)} %get-tuple-element.33.c_ref, bf16[704,1024]{1,0:T(8,128)(2,1)} %bitcast.59, ...), custom_call_target="tpu_custom_call" | custom-call | flops 27000000512 | bytes 30000000 | tf_op jit(solution)/shard_map/middle/pallas_call | solution.py:857
  123.9 188.9 %after.1 = (bf16[2,256,1024]{2,1,0:T(8,128)(2,1)}, bf16[2,256,1024]{2,1,0:T(8,128)(2,1)}, bf16[136,16,1024]{2,1,0:T(8,128)(2,1)}, bf16[32,128,128]{2,1,0:T(8,128...) custom-call(bf16[136,16,1024]{2,1,0:T(8,128)(2,1)} %get-tuple-elemen, ...), custom_call_target="tpu_custom_call" | custom-call | flops 60000002048 | bytes 60000000 | tf_op jit(solution)/shard_map/after/pallas_call | solution.py:1164
  312.9 1.7 convert_bitcast_fusion.1
  314.6 1.0 copy.23
  315.6 0.8 copy.30
  316.4 0.6 fusion.1
  317.0 1.9 slice_bitcast_fusion
  319.0 0.0 copy-done.4
  319.0 0.5 copy-done.5
  319.5 0.5 convert_bitcast_fusion
  320.0 2.4 copy.24
  322.4 0.0 slice-start
  322.4 0.0 slice-start.1
  322.5 3.0 copy.29
  325.5 0.5 fusion
  326.0 2.0 bitcast_convert_fusion
  328.0 3.4 %convert_bitcast_fusion.2 = (f32[1024,704]{0,1:T(8,128)}, f32[1024,704]{0,1:T(8,128)}) fusion(bf16[44,16,1024]{2,1,0:T(8,128)(2,1)S(1)} %get-tuple-element.56, bf16[44,16,1024]{2,1,0:T(8,128)(2,1)S(1)} %get-tuple-element.57), kind=kLoop, calls=%fused_computation.5 | loop fusion | flops 1441792 | bytes 8650752 | tf_op jit(solution)/shard_map/transpose | solution.py:1242
  331.4 1.0 copy.33
  332.4 1.0 copy.34
  (13 shorter events, 0.0 us)
Async XLA Ops:
  0.6 0.7 copy-start
  317.0 1.9 copy-start.4
  317.0 2.5 copy-start.5
  322.4 3.1 slice-start
  322.4 3.1 slice-start.1
  328.0 3.4 %copy-start.3 = (bf16[2,256,1024]{2,1,0:T(8,128)(2,1)S(1)}, bf16[2,256,1024]{2,1,0:T(8,128)(2,1)}, u32[]{:S(2)}) copy-start(bf16[2,256,1024]{2,1,0:T(8,128)(2,1)} %get-tuple-element.71) | copy-start | bytes 3145732
  328.0 4.4 %copy-start.2 = (bf16[2,256,1024]{2,1,0:T(8,128)(2,1)S(1)}, bf16[2,256,1024]{2,1,0:T(8,128)(2,1)}, u32[]{:S(2)}) copy-start(bf16[2,256,1024]{2,1,0:T(8,128)(2,1)} %get-tuple-element.72) | copy-start | bytes 3145732
  328.0 5.4 %copy-start.1 = (s32[2,1024]{1,0:T(2,128)S(1)}, s32[2,1024]{1,0:T(2,128)}, u32[]{:S(2)}) copy-start(s32[2,1024]{1,0:T(2,128)} %param.11) | copy-start | bytes 24580
